TPU v7x, 32 devices: a whole 2x2x4 slice. The times are simulated.
32 devices in a mesh: lon: 8 (over z, x), lat: 4 (over y, core).
Axes of the slice: x: 2, y: 2, z: 4, core: 2. Of those that a mesh axis runs over, the one named last changes fastest.
Arguments:
- field: float32 [2, 128, 512], P(None, 'lat', 'lon'), may hold values from -6 to 6
- gamma: float32 [2, 128, 512], P(None, 'lat', 'lon'), may hold values from 1 to 192
- kappa_zonal: float32 [2, 128, 512], P(None, 'lat', 'lon'), may hold values from 4096 to 49152
- kappa_merid: float32 [2, 128, 512], P(None, 'lat', 'lon'), may hold values from 1024 to 12288
- area: float32 [128, 512], P('lat', 'lon'), may hold values from 0.3 to 3
- sea_mask: int32 [128, 512], P('lat', 'lon'), may hold values from 0 to 1, as said below
- fold_pair: int32 [512], P('lon'), may hold values from 0 to 511, as said below
Outputs:
- covaried: float32 [2, 128, 512], P(None, 'lat', 'lon')
Inputs may be any that keep to these rules, and one draw needn't show every extreme that they name: `sea_mask`: ocean cells are 1 and land cells 0; land comes in rectangles, periodic in longitude. A mirror pairing across the fold: fold_pair[i] + i is the same odd number modulo 512 for every i, so fold_pair[fold_pair[i]] == i and fold_pair[i] != i.
All inputs are finite; a program needn't handle non-finite values.
Results may differ from a plain program's by a relative error of at most 0.00095.
Values sent between devices are 32-bit elements; how exact they have to be, the bound alone decides.
No kernel may reach another device: no remote copies, remote signals or barrier semaphores. Data moves between devices by JAX's collectives and lax.ppermute only.
A program may use at most 64 MiB of HBM per device.

v0:
```python
import jax
import jax.numpy as jnp
from jax import lax
from jax.sharding import PartitionSpec as P


def passed_along(block, axis, distance):
    devices = range(lax.axis_size(axis))
    route = [((i - distance) % len(devices), i) for i in devices]
    return lax.ppermute(block, axis, route)


def passed_along_2(value, axis, by):
    size = lax.axis_size(axis)
    pairs = [(i, i + by) for i in range(size) if 0 <= i + by < size]
    return lax.ppermute(value, axis, pairs)


def slide(values, offset, fill, wrap):
    if wrap:
        return jnp.roll(values, offset, axis=-1)
    edge = jnp.full(values.shape[:-1] + (abs(offset),), fill, values.dtype)
    if offset > 0:
        return jnp.concatenate([edge, values[..., :-offset]], axis=-1)
    return jnp.concatenate([values[..., -offset:], edge], axis=-1)


def reduce_lines(lower, diagonal, upper, source, wrap):
    length = source.shape[-1]
    stride = 1
    while stride < length:
        below_diag = slide(diagonal, stride, 1.0, wrap)
        above_diag = slide(diagonal, -stride, 1.0, wrap)
        factor_low = -lower / below_diag
        factor_up = -upper / above_diag
        new_diagonal = (
            diagonal
            + factor_low * slide(upper, stride, 0.0, wrap)
            + factor_up * slide(lower, -stride, 0.0, wrap)
        )
        source = (
            source
            + factor_low * slide(source, stride, 0.0, wrap)
            + factor_up * slide(source, -stride, 0.0, wrap)
        )
        lower = factor_low * slide(lower, stride, 0.0, wrap)
        upper = factor_up * slide(upper, -stride, 0.0, wrap)
        diagonal = new_diagonal
        stride = stride * 2
    if wrap:
        return source / (diagonal + lower + upper)
    return source / diagonal


def cyclic_solve(faces, source):
    before = jnp.roll(faces, 1, axis=-1)
    diagonal = 1.0 + before + faces
    return reduce_lines(-before, diagonal, -faces, source, True)


def open_solve(faces, source):
    before = jnp.concatenate([jnp.zeros_like(faces[..., :1]), faces[..., :-1]], axis=-1)
    diagonal = 1.0 + before + faces
    upper_band = jnp.concatenate([-faces[..., :-1], jnp.zeros_like(faces[..., :1])], axis=-1)
    return reduce_lines(-before, diagonal, upper_band, source, False)


def to_columns(blocks, lanes):
    levels, height, breadth = blocks.shape
    split = blocks.reshape(levels, height, lanes, breadth // lanes)
    return jnp.transpose(split, (2, 0, 3, 1))


def from_columns(pieces):
    lanes, levels, narrow, height = pieces.shape
    return jnp.transpose(pieces, (1, 3, 0, 2)).reshape(levels, height, lanes * narrow)


def local(field, gamma, kappa_zonal, kappa_merid, area, sea_mask, fold_pair):
    ocean_cells = sea_mask.astype(jnp.float32)
    east_edge = passed_along(ocean_cells[:, :1], "lon", -1)
    north_edge = passed_along_2(ocean_cells[:1, :], "lat", -1)
    east_ocean = jnp.concatenate([ocean_cells[:, 1:], east_edge], axis=1)
    north_ocean = jnp.concatenate([ocean_cells[1:], north_edge], axis=0)
    zonal_faces = kappa_zonal * (ocean_cells * east_ocean)[None]
    merid_faces = kappa_merid * (ocean_cells * north_ocean)[None]
    scaled = gamma * ocean_cells[None]
    lanes = lax.axis_size("lat")
    zonal_lines = lax.all_to_all(zonal_faces, "lon", split_axis=1, concat_axis=2, tiled=True)
    merid_lines = lax.all_to_all(
        to_columns(merid_faces, lanes), "lat", split_axis=0, concat_axis=3, tiled=True
    )[0]

    def zonal_pass(current):
        lines = lax.all_to_all(current, "lon", split_axis=1, concat_axis=2, tiled=True)
        return lax.all_to_all(
            cyclic_solve(zonal_lines, lines), "lon", split_axis=2, concat_axis=1, tiled=True
        )

    def merid_open(current):
        return lax.all_to_all(
            to_columns(current, lanes), "lat", split_axis=0, concat_axis=3, tiled=True
        )[0]

    def merid_close(columns):
        return from_columns(
            lax.all_to_all(columns[None], "lat", split_axis=3, concat_axis=0, tiled=True)
        )

    current = zonal_pass(scaled * field)
    columns = open_solve(merid_lines, merid_open(current))
    current = merid_close(columns)
    is_top = lax.axis_index("lat") == lanes - 1

    def fold_natural(values):
        top_cells = values[:, -1, :]
        whole_row = lax.all_gather(top_cells, "lon", axis=1, tiled=True)
        partner = jnp.take(whole_row, fold_pair, axis=1)
        return values.at[:, -1, :].set(jnp.where(is_top, 0.5 * (top_cells + partner), top_cells))

    current = fold_natural(current)
    current = current / area[None]
    current = fold_natural(current)
    current = merid_close(open_solve(merid_lines, merid_open(current)))
    current = zonal_pass(current)
    return scaled * current


def solution(mesh):
    return jax.shard_map(
        local,
        mesh=mesh,
        in_specs=(
            P(None, "lat", "lon"),
            P(None, "lat", "lon"),
            P(None, "lat", "lon"),
            P(None, "lat", "lon"),
            P("lat", "lon"),
            P("lat", "lon"),
            P("lon"),
        ),
        out_specs=P(None, "lat", "lon"),
        check_vma=False,
    )
```

profile of v0, /device:TPU:0, one launch (start us, length us, event | category | flops | bytes accessed | tf_op | source)
XLA Modules:
  0.0 188.0 jit_solution(8956095462419415965)
XLA Ops:
  0.7 1.4 collective-permute-start.1
  2.1 6.0 %collective-permute-start = (f32[32,1]{1,0:T(8,128)S(1)}, f32[32,1]{1,0:T(8,128)S(1)}, u32[]{:S(2)}, u32[]{:S(2)}) collective-permute-start(f32[32,1]{1,0:T(8,128)S(1)} %bitcast.116), channel_id=1, source_target_pairs={{4,0},{8,4},{12,8},{16,12},{20,16},{24,20},{28,24},{0,28},{5,1},{9... | collective-permute-start | bytes 392 | tf_op jit(solution)/shard_map/ppermute | solution.py:10
  11.4 3.5 %all-to-all-start.4 = ((f32[4,1,1024]{2,1,0:T(1,128)}), f32[4,1,1024]{2,1,0:T(1,128)S(1)}, u32[]{:S(2)}, u32[]{:S(2)}) async-start(f32[4,1,1024]{2,1,0:T(1,128)} %reshape.120), calls=%async_computation.4 | async-start | bytes 32768 | tf_op jit(solution)/shard_map/all_to_all | solution.py:90
  15.7 3.1 %all-to-all-done.4 = f32[4,1,1024]{2,1,0:T(1,128)S(1)} async-done(((f32[4,1,1024]{2,1,0:T(1,128)}), f32[4,1,1024]{2,1,0:T(1,128)S(1)}, u32[]{:S(2)}, u32[]{:S(2)}) %all-to-all-start.4) | async-done | bytes 16416 | tf_op jit(solution)/shard_map/all_to_all | solution.py:90
  18.8 5.4 %all-to-all-start = ((f32[8,1,512]{2,1,0:T(1,128)}), f32[8,1,512]{2,1,0:T(1,128)S(1)}, u32[]{:S(2)}, u32[]{:S(2)}) async-start(f32[8,1,512]{2,1,0:T(1,128)} %reshape.122), calls=%async_computation | async-start | bytes 32768 | tf_op jit(solution)/shard_map/all_to_all | solution.py:95
  24.8 0.7 reduce.8
  25.8 4.9 %all-to-all-done = f32[8,1,512]{2,1,0:T(1,128)S(1)} async-done(((f32[8,1,512]{2,1,0:T(1,128)}), f32[8,1,512]{2,1,0:T(1,128)S(1)}, u32[]{:S(2)}, u32[]{:S(2)}) %all-to-all-start) | async-done | bytes 16416 | tf_op jit(solution)/shard_map/all_to_all | solution.py:95
  30.8 3.3 %all-to-all-start.1 = ((f32[8,1,512]{2,1,0:T(1,128)}), f32[8,1,512]{2,1,0:T(1,128)S(1)}, u32[]{:S(2)}, u32[]{:S(2)}) async-start(f32[8,1,512]{2,1,0:T(1,128)} %reshape.124), calls=%async_computation.1 | async-start | bytes 32768 | tf_op jit(solution)/shard_map/all_to_all | solution.py:89
  34.1 0.7 reduce.5
  35.2 5.4 %all-to-all-done.1 = f32[8,1,512]{2,1,0:T(1,128)S(1)} async-done(((f32[8,1,512]{2,1,0:T(1,128)}), f32[8,1,512]{2,1,0:T(1,128)S(1)}, u32[]{:S(2)}, u32[]{:S(2)}) %all-to-all-start.1) | async-done | bytes 16416 | tf_op jit(solution)/shard_map/all_to_all | solution.py:89
  48.2 1.3 reshape.126
  49.5 3.3 %all-to-all-start.2 = ((f32[8,1,512]{2,1,0:T(1,128)}), f32[8,1,512]{2,1,0:T(1,128)S(1)}, u32[]{:S(2)}, u32[]{:S(2)}) async-start(f32[8,1,512]{2,1,0:T(1,128)} %reshape.126), calls=%async_computation.2 | async-start | bytes 32768 | tf_op jit(solution)/shard_map/all_to_all | solution.py:96
  52.9 6.4 %all-to-all-done.2 = f32[8,1,512]{2,1,0:T(1,128)S(1)} async-done(((f32[8,1,512]{2,1,0:T(1,128)}), f32[8,1,512]{2,1,0:T(1,128)S(1)}, u32[]{:S(2)}, u32[]{:S(2)}) %all-to-all-start.2) | async-done | bytes 16416 | tf_op jit(solution)/shard_map/all_to_all | solution.py:96
  60.1 0.8 reshape.127
  62.1 3.3 %all-to-all-start.3 = ((f32[4,1,1024]{2,1,0:T(1,128)}), f32[4,1,1024]{2,1,0:T(1,128)S(1)}, u32[]{:S(2)}, u32[]{:S(2)}) async-start(f32[4,1,1024]{2,1,0:T(1,128)} %reshape.128), calls=%async_computation.3 | async-start | bytes 32768 | tf_op jit(solution)/shard_map/all_to_all | solution.py:101
  65.4 3.7 %all-to-all-done.3 = f32[4,1,1024]{2,1,0:T(1,128)S(1)} async-done(((f32[4,1,1024]{2,1,0:T(1,128)}), f32[4,1,1024]{2,1,0:T(1,128)S(1)}, u32[]{:S(2)}, u32[]{:S(2)}) %all-to-all-start.3) | async-done | bytes 16416 | tf_op jit(solution)/shard_map/all_to_all | solution.py:101
  69.2 0.7 reduce.7
  73.3 0.8 reshape.130
  74.1 3.3 %all-to-all-start.5 = ((f32[4,1,1024]{2,1,0:T(1,128)}), f32[4,1,1024]{2,1,0:T(1,128)S(1)}, u32[]{:S(2)}, u32[]{:S(2)}) async-start(f32[4,1,1024]{2,1,0:T(1,128)} %reshape.130), calls=%async_computation.5 | async-start | bytes 32768 | tf_op jit(solution)/shard_map/all_to_all | solution.py:107
  77.4 3.8 %all-to-all-done.5 = f32[4,1,1024]{2,1,0:T(1,128)S(1)} async-done(((f32[4,1,1024]{2,1,0:T(1,128)}), f32[4,1,1024]{2,1,0:T(1,128)S(1)}, u32[]{:S(2)}, u32[]{:S(2)}) %all-to-all-start.5) | async-done | bytes 16416 | tf_op jit(solution)/shard_map/all_to_all | solution.py:107
  81.2 0.7 reduce.9
  82.2 1.0 copy.77
  83.3 30.8 %all-gather = f32[2,1,512]{0,2,1:T(8,128)S(1)} all-gather(f32[2,1,64]{0,2,1:T(8,128)S(1)} %slice.1420), channel_id=2, replica_groups=mesh['lon'=8,'lat'=4] {'lon'}, dimensions={2}, use_global_device_ids=true | all-gather | bytes 4608 | tf_op jit(solution)/shard_map/all_gather | solution.py:117
  115.7 30.7 %all-gather.1 = f32[2,1,512]{0,2,1:T(8,128)S(1)} all-gather(f32[2,1,64]{0,2,1:T(8,128)S(1)} %slice.1421), channel_id=3, replica_groups=mesh['lon'=8,'lat'=4] {'lon'}, dimensions={2}, use_global_device_ids=true | all-gather | bytes 4608 | tf_op jit(solution)/shard_map/all_gather | solution.py:117
  147.9 6.2 %all_to_all.168 = f32[4,1,1024]{2,1,0:T(1,128)S(1)} all-to-all(f32[4,1,1024]{2,1,0:T(1,128)S(1)} %reshape.132), channel_id=1, replica_groups=mesh['lon'=8,'lat'=4] {'lat'}, dimensions={0} | all-to-all | bytes 32768 | tf_op jit(solution)/shard_map/all_to_all | solution.py:101
  154.1 0.7 reduce.10
  156.5 6.2 %all_to_all.169 = f32[4,1,1024]{2,1,0:T(1,128)S(1)} all-to-all(f32[4,1,1024]{2,1,0:T(1,128)S(1)} %reshape.134), channel_id=1, replica_groups=mesh['lon'=8,'lat'=4] {'lat'}, dimensions={0} | all-to-all | bytes 32768 | tf_op jit(solution)/shard_map/all_to_all | solution.py:107
  162.7 0.7 reduce.11
  164.0 8.9 %all_to_all.170 = f32[8,1,512]{2,1,0:T(1,128)S(1)} all-to-all(f32[8,1,512]{2,1,0:T(1,128)S(1)} %reshape.136), channel_id=1, replica_groups=mesh['lon'=8,'lat'=4] {'lon'}, dimensions={0} | all-to-all | bytes 32768 | tf_op jit(solution)/shard_map/all_to_all | solution.py:95
  175.9 0.7 reshape.138
  176.6 8.9 %all_to_all.171 = f32[8,1,512]{2,1,0:T(1,128)S(1)} all-to-all(f32[8,1,512]{2,1,0:T(1,128)S(1)} %reshape.138), channel_id=1, replica_groups=mesh['lon'=8,'lat'=4] {'lon'}, dimensions={0} | all-to-all | bytes 32768 | tf_op jit(solution)/shard_map/all_to_all | solution.py:96
  186.3 0.8 reshape.139
  (261 shorter events, 28.4 us)
Async XLA Ops:
  0.7 7.5 %copy-start.6 = (s32[64]{0:T(128)S(1)}, s32[64]{0:T(128)}, u32[]{:S(2)}) copy-start(s32[64]{0:T(128)} %param.19) | copy-start | bytes 772
  0.7 9.2 %collective-permute-start.1 = (f32[1,64]{1,0:T(1,128)S(1)}, f32[1,64]{1,0:T(1,128)S(1)}, u32[]{:S(2)}, u32[]{:S(2)}) collective-permute-start(f32[1,64]{1,0:T(1,128)S(1)} %slice.1367), channel_id=1, source_target_pairs={{1,0},{2,1},{3,2},{5,4},{6,5},{7,6},{9,8},{10,9},{11,10},{13,12},{... | collective-permute-start | bytes 776 | tf_op jit(solution)/shard_map/ppermute | solution.py:16
  2.1 7.7 %collective-permute-start = (f32[32,1]{1,0:T(8,128)S(1)}, f32[32,1]{1,0:T(8,128)S(1)}, u32[]{:S(2)}, u32[]{:S(2)}) collective-permute-start(f32[32,1]{1,0:T(8,128)S(1)} %bitcast.116), channel_id=1, source_target_pairs={{4,0},{8,4},{12,8},{16,12},{20,16},{24,20},{28,24},{0,28},{5,1},{9... | collective-permute-start | bytes 392 | tf_op jit(solution)/shard_map/ppermute | solution.py:10
  8.2 0.8 copy-start
  8.2 0.8 copy-start.2
  9.0 0.8 copy-start.3
  9.8 0.7 copy-start.1
  11.4 3.6 %copy-start.4 = (f32[2,32,64]{2,1,0:T(8,128)S(1)}, f32[2,32,64]{2,1,0:T(8,128)}, u32[]{:S(2)}) copy-start(f32[2,32,64]{2,1,0:T(8,128)} %param.15) | copy-start | bytes 49156
  11.4 7.4 %all-to-all-start.4 = ((f32[4,1,1024]{2,1,0:T(1,128)}), f32[4,1,1024]{2,1,0:T(1,128)S(1)}, u32[]{:S(2)}, u32[]{:S(2)}) async-start(f32[4,1,1024]{2,1,0:T(1,128)} %reshape.120), calls=%async_computation.4 | async-start | bytes 32768 | tf_op jit(solution)/shard_map/all_to_all | solution.py:90
  18.8 12.0 %all-to-all-start = ((f32[8,1,512]{2,1,0:T(1,128)}), f32[8,1,512]{2,1,0:T(1,128)S(1)}, u32[]{:S(2)}, u32[]{:S(2)}) async-start(f32[8,1,512]{2,1,0:T(1,128)} %reshape.122), calls=%async_computation | async-start | bytes 32768 | tf_op jit(solution)/shard_map/all_to_all | solution.py:95
  30.8 9.9 %all-to-all-start.1 = ((f32[8,1,512]{2,1,0:T(1,128)}), f32[8,1,512]{2,1,0:T(1,128)S(1)}, u32[]{:S(2)}, u32[]{:S(2)}) async-start(f32[8,1,512]{2,1,0:T(1,128)} %reshape.124), calls=%async_computation.1 | async-start | bytes 32768 | tf_op jit(solution)/shard_map/all_to_all | solution.py:89
  49.5 9.9 %all-to-all-start.2 = ((f32[8,1,512]{2,1,0:T(1,128)}), f32[8,1,512]{2,1,0:T(1,128)S(1)}, u32[]{:S(2)}, u32[]{:S(2)}) async-start(f32[8,1,512]{2,1,0:T(1,128)} %reshape.126), calls=%async_computation.2 | async-start | bytes 32768 | tf_op jit(solution)/shard_map/all_to_all | solution.py:96
  62.1 7.1 %all-to-all-start.3 = ((f32[4,1,1024]{2,1,0:T(1,128)}), f32[4,1,1024]{2,1,0:T(1,128)S(1)}, u32[]{:S(2)}, u32[]{:S(2)}) async-start(f32[4,1,1024]{2,1,0:T(1,128)} %reshape.128), calls=%async_computation.3 | async-start | bytes 32768 | tf_op jit(solution)/shard_map/all_to_all | solution.py:101
  74.1 7.1 %all-to-all-start.5 = ((f32[4,1,1024]{2,1,0:T(1,128)}), f32[4,1,1024]{2,1,0:T(1,128)S(1)}, u32[]{:S(2)}, u32[]{:S(2)}) async-start(f32[4,1,1024]{2,1,0:T(1,128)} %reshape.130), calls=%async_computation.5 | async-start | bytes 32768 | tf_op jit(solution)/shard_map/all_to_all | solution.py:107
  114.7 0.7 copy-start.5
where the time goes:
time: 189 us; the launch traced here: 188 us
  blocking collectives  91.9 us (49%)
  starting transfers between devices  29.6 us (16%)
  waiting for transfers between devices  27.5 us (15%)
  local copies, waits for them, and re-layouts  24.2 us (13%)
  other arithmetic  14 us (7%)
    all_gather x2, blocking collectives, fold_natural(): whole_row = lax.all_gather(top_cells, 'lon', axis=1, tiled=True)  61.6 us
    unnamed x35, local copies, waits for them, and re-layouts  10.7 us
    all_to_all x1, blocking collectives, zonal_pass(): lax.all_to_all(current, 'lon', split_axis=1, concat_axis=2, tiled=True)  8.94 us
    all_to_all x1, blocking collectives, zonal_pass(): lax.all_to_all(cyclic_solve(zonal_lines, lines), 'lon', split_axis=2, con...  8.94 us
    all_to_all x1, waiting for transfers between devices, zonal_pass(): lax.all_to_all(cyclic_solve(zonal_lines, lines), 'lon', split_axis=2, con...  6.44 us
    all_to_all x1, blocking collectives, merid_open(): lax.all_to_all(to_columns(current, lanes), 'lat', split_axis=0, concat_ax...  6.21 us
    all_to_all x1, blocking collectives, merid_close(): lax.all_to_all(columns[None], 'lat', split_axis=3, concat_axis=0, tiled=T...  6.21 us
    ppermute x1, starting transfers between devices, passed_along(): return lax.ppermute(block, axis, route)  6.03 us
  transfers between devices with their start and end apart: 8, of which 6 were waited for; matrix products, arithmetic and copies ran while one was open for 2% of the time, Pallas kernels for 0%

commit v1 on v0

v1 whole, which is shorter than its diff:
```python
import functools

import jax
import jax.numpy as jnp
from jax import lax
from jax.experimental import pallas as pl
from jax.experimental.pallas import tpu as pltpu
from jax.sharding import PartitionSpec as P


F32 = jnp.float32
EXACT = lax.Precision.HIGHEST


def moved(values, distance, axis):
    return pltpu.roll(values, distance % values.shape[axis], axis)


def iota(shape, axis):
    return lax.broadcasted_iota(jnp.int32, shape, axis)


def spread(values, up, down, stride, axis):
    return values + moved(up * values, stride, axis) + moved(down * values, -stride, axis)


def condense(left, right, totals, count, axis):
    factors = []
    stride = 1
    while stride < count:
        pull = 1.0 / (totals[0] + left + right)
        up, down = right * pull, left * pull
        link = left * up
        factors.append((up, down))
        totals = [spread(t, up, down, stride, axis) for t in totals]
        left, right = moved(link, stride, axis), moved(link, -stride, axis)
        stride *= 2
    return factors, totals


def relax(values, factors, axis):
    stride = 1
    for up, down in factors:
        values = spread(values, up, down, stride, axis)
        stride *= 2
    return values


def load_factors(ref):
    return [(ref[2 * k], ref[2 * k + 1]) for k in range(ref.shape[0] // 2)]


def store_factors(ref, factors):
    for k, (up, down) in enumerate(factors):
        ref[2 * k] = up
        ref[2 * k + 1] = down


def beside(ref):
    return jnp.concatenate([ref[k] for k in range(ref.shape[0])], axis=-1)


def chain(faces, place, length, axis):
    inner = (place >= 1) & (place <= length - 3)
    right = jnp.where(inner, faces, 0.0)
    left = moved(right, 1, axis)
    to_first = jnp.where(place == 1, moved(faces, 1, axis), 0.0)
    to_last = jnp.where(place == length - 2, faces, 0.0)
    return left, right, to_first, to_last


def half_sums(arrays, levels):
    wide = jnp.concatenate(arrays, axis=1)
    lanes = arrays[0].shape[1]
    width = lanes // levels
    shape = (8 * levels, wide.shape[1])
    row, col = iota(shape, 0), iota(shape, 1)
    pick = ((col // lanes == row % 8) & (col % lanes // width == row // 8)).astype(F32)
    sums = lax.dot_general(pick, wide, (((1,), (1,)), ((), ())), precision=EXACT, preferred_element_type=F32)
    return jnp.concatenate([sums[8 * k : 8 * k + 8] for k in range(levels)], axis=1)


def padded(rows, lanes):
    return jnp.concatenate([rows, jnp.zeros((rows.shape[0], lanes - rows.shape[1]), F32)], axis=1)


def zonal_local(field, gamma, kappa, mask, message, factors_out, out):
    levels, height, width = field.shape
    ocean = mask[...].astype(F32)
    ocean = jnp.concatenate([ocean] * levels, axis=1)
    lanes = levels * width
    place = iota((height, lanes), 1) % width
    scaled = beside(gamma) * ocean
    source = scaled * beside(field)
    open_face = beside(kappa) * ocean
    faces = open_face * moved(ocean, -1, 1)
    left, right, to_first, to_last = chain(faces, place, width, 1)
    factors, (ground, first, last) = condense(
        left, right, [1.0 + to_first + to_last, to_first, to_last], width - 2, 1
    )
    inverse = 1.0 / ground
    first = first * inverse
    last = last * inverse
    edge = to_first * last
    first_full = jnp.where(place == 0, 1.0, first)
    last_full = jnp.where(place == width - 1, 1.0, last)
    rows = half_sums(
        [
            first_full * source,
            last_full * source,
            first_full,
            last_full,
            edge,
            jnp.where(place == width - 1, open_face, 0.0),
            jnp.where(place == 0, ocean, 0.0),
        ],
        levels,
    )
    message[...] = jnp.broadcast_to(padded(rows, message.shape[2])[None], message.shape)
    store_factors(factors_out, factors)
    inner = (place >= 1) & (place <= width - 2)
    out[0] = first_full
    out[1] = last_full
    out[2] = jnp.where(inner, inverse, 0.0)
    out[3] = source
    out[4] = scaled


def merid_local(zonal_factors, zonal, kappa, area, mask, direct, factors_out, out, rows_out):
    levels, height, width = kappa.shape
    ocean = mask[...].astype(F32)
    ocean = jnp.concatenate([ocean] * levels, axis=1)
    reciprocal = 1.0 / area[...]
    reciprocal = jnp.concatenate([reciprocal] * levels, axis=1)
    lanes = levels * width
    row = iota((height, lanes), 0)
    open_face = beside(kappa) * ocean
    faces = open_face * moved(ocean, -1, 0)
    left, right, to_first, to_last = chain(faces, row, height, 0)
    factors, (ground, first, last) = condense(
        left, right, [1.0 + to_first + to_last, to_first, to_last], height - 2, 0
    )
    inner = (row >= 1) & (row <= height - 2)
    inverse = jnp.where(inner, 1.0 / ground, 0.0)
    first = first * inverse
    last = last * inverse
    edge = jnp.sum(to_first * last, axis=0, keepdims=True)
    again_first = relax(first * reciprocal, factors, 0) * inverse
    again_last = relax(last * reciprocal, factors, 0) * inverse
    first = jnp.where(row == 0, 1.0, first)
    last = jnp.where(row == height - 1, 1.0, last)

    def total(values):
        return jnp.sum(values, axis=0, keepdims=True)

    rows = [
        total(first),
        total(last),
        edge,
        open_face[height - 1 :],
        ocean[:1],
        total(first * first * reciprocal),
        total(first * last * reciprocal),
        total(jnp.where(row == height - 1, 0.0, last * last * reciprocal)),
        reciprocal[height - 1 :],
    ]
    rows_out[...] = jnp.concatenate([jnp.zeros((4, lanes), F32)] + rows + [jnp.zeros((3, lanes), F32)], axis=0)
    store_factors(factors_out, factors)
    out[0] = first
    out[1] = last
    out[2] = again_first
    out[3] = again_last
    out[4] = inverse
    out[5] = reciprocal
    direct[...] = relax(zonal[3] * (zonal[2] > 0.0), load_factors(zonal_factors), 1) * zonal[2]


def own_columns(values, index, height, levels, lanes):
    own = jnp.sum(jnp.where(iota(values.shape, 0) == index, values, 0.0), axis=0, keepdims=True)
    shape = (height, values.shape[1])
    row, col = iota(shape, 0), iota(shape, 1)
    columns = [
        jnp.sum(jnp.where(col == row + k * height, own, 0.0), axis=1, keepdims=True) for k in range(levels)
    ]
    lane = iota((height, lanes), 1)
    width = lanes // levels
    result = jnp.broadcast_to(columns[0], (height, lanes))
    for k in range(1, levels):
        result = jnp.where(lane >= k * width, columns[k], result)
    return result


def ring_ends(first_source, last_source, edge_pull, face_pull, last_pull, factors, inverse):
    values = first_source + edge_pull * last_source + moved(face_pull * last_source, 1, 0)
    first = relax(values, factors, 0) * inverse
    last = last_pull * last_source + edge_pull * first + face_pull * moved(first, -1, 0)
    return first, last


def zonal_join(gathered, zonal, direct, merid, merid_rows, current_out, message, ring):
    levels = 2
    height, lanes = direct.shape
    index = lax.axis_index("lon")
    first_source, last_source, first_ground, last_ground, edge, open_face, ocean = [
        gathered[:, k, :] for k in range(7)
    ]
    devices = edge.shape[0]
    used = iota(edge.shape, 1) < levels * height
    first_ground = jnp.where(used, first_ground, 1.0)
    last_ground = jnp.where(used, last_ground, 1.0)
    face = open_face * moved(ocean, -1, 0)
    last_pull = 1.0 / (last_ground + edge + face)
    edge_pull, face_pull = edge * last_pull, face * last_pull
    ground = first_ground + edge_pull * last_ground + moved(face_pull * last_ground, 1, 0)
    link = edge * face_pull
    factors, (ground,) = condense(moved(link, 1, 0), link, [ground], devices, 0)
    inverse = 1.0 / ground
    first, last = ring_ends(first_source, last_source, edge_pull, face_pull, last_pull, factors, inverse)
    ring[0] = edge_pull
    ring[1] = face_pull
    ring[2] = last_pull
    ring[3] = inverse
    for k, (up, down) in enumerate(factors):
        ring[4 + 2 * k] = up
        ring[5 + 2 * k] = down
    current = (
        direct[...]
        + zonal[0] * own_columns(first, index, height, levels, lanes)
        + zonal[1] * own_columns(last, index, height, levels, lanes)
    )
    current_out[...] = current
    rows = [jnp.sum(merid[k] * current, axis=0, keepdims=True) for k in range(4)]
    whole = jnp.concatenate(rows + [merid_rows[4:]], axis=0)
    message[...] = jnp.broadcast_to(whole[None], message.shape)


def merid_twice(current, factors_ref, merid, out):
    factors = load_factors(factors_ref)
    inner = merid[4] > 0.0
    once = relax(jnp.where(inner, current[...], 0.0), factors, 0) * merid[4]
    out[...] = relax(once * merid[5], factors, 0) * merid[4]


def line_factors(left, right, ground):
    count = len(ground)
    factors = []
    stride = 1
    while stride < count:
        pull = [1.0 / (ground[k] + left[k] + right[k]) for k in range(count)]
        up = [right[k] * pull[k] for k in range(count)]
        down = [left[k] * pull[k] for k in range(count)]
        link = [left[k] * up[k] for k in range(count)]
        factors.append((up, down))
        ground = line_relax(ground, [factors[-1]], stride)
        zero = jnp.zeros_like(link[0])
        left = [link[k - stride] if k >= stride else zero for k in range(count)]
        right = [link[k + stride] if k + stride < count else zero for k in range(count)]
        stride *= 2
    return factors, ground


def line_relax(values, factors, stride=1):
    count = len(values)
    for up, down in factors:
        fresh = []
        for k in range(count):
            value = values[k]
            if k >= stride:
                value = value + up[k - stride] * values[k - stride]
            if k + stride < count:
                value = value + down[k + stride] * values[k + stride]
            fresh.append(value)
        values = fresh
        stride *= 2
    return values


def mirrored(values, pivot, width, levels):
    count, devices, lanes = values.shape
    pivot_block, pivot_place = pivot // width, pivot % width
    shape = (lanes, lanes)
    source, target = iota(shape, 0), iota(shape, 1)
    reach = pivot_place - target % width
    same = source // width == target // width
    flat = values.reshape(count * devices, lanes)
    result = 0.0
    for extra in range(2):
        lane_pick = (same & (source % width == reach + extra * width)).astype(F32)
        turned = lax.dot(flat, lane_pick, precision=EXACT, preferred_element_type=F32)
        shape = (count * devices, count * devices)
        goal, origin = iota(shape, 0), iota(shape, 1)
        wanted = (pivot_block - goal % devices - extra + 2 * devices) % devices
        block_pick = ((goal // devices == origin // devices) & (origin % devices == wanted)).astype(F32)
        result = result + lax.dot(block_pick, turned, precision=EXACT, preferred_element_type=F32)
    return result.reshape(values.shape)


def merid_join(gathered, again, merid, zonal, pairing, current_out, message):
    levels = 2
    height, lanes = again.shape
    width = lanes // levels
    devices_x, devices_y = gathered.shape[:2]
    index_x, index_y = lax.axis_index("lon"), lax.axis_index("lat")
    pivot = (pairing[0] + index_x * width) % (devices_x * width)

    def part(k):
        return [gathered[:, y, k, :] for y in range(devices_y)]

    (first_source, last_source, first_again, last_again, first_ground, last_ground, edge, open_face, ocean,
     first_first, first_last, last_last, reciprocal) = [part(k) for k in range(13)]
    lats = range(devices_y)
    top = devices_y - 1
    face = [open_face[y] * ocean[y + 1] if y < top else jnp.zeros_like(edge[y]) for y in lats]
    last_pull = [1.0 / (last_ground[y] + edge[y] + face[y]) for y in lats]
    edge_pull = [edge[y] * last_pull[y] for y in lats]
    face_pull = [face[y] * last_pull[y] for y in lats]
    below = lambda values: [values[y - 1] if y > 0 else jnp.zeros_like(values[0]) for y in lats]

    def gather_to_first(first_values, last_values):
        up = below([face_pull[y] * last_values[y] for y in lats])
        return [first_values[y] + edge_pull[y] * last_values[y] + up[y] for y in lats]

    link = [edge[y] * face_pull[y] for y in lats]
    factors, ground = line_factors(below(link), link, gather_to_first(first_ground, last_ground))
    inverse = [1.0 / g for g in ground]

    def ends(first_values, last_values):
        relaxed = line_relax(gather_to_first(first_values, last_values), factors)
        first = [relaxed[y] * inverse[y] for y in lats]
        last = []
        for y in lats:
            value = last_pull[y] * last_values[y] + edge_pull[y] * first[y]
            if y < top:
                value = value + face_pull[y] * first[y + 1]
            last.append(value)
        return first, last

    first_one, last_one = ends(first_source, last_source)
    across = mirrored(jnp.stack([last_one[top], reciprocal[top]]), pivot, width, levels)
    folded = 0.25 * (last_one[top] + across[0]) * (reciprocal[top] + across[1])
    first_next = [
        first_again[y] + first_first[y] * first_one[y] + first_last[y] * last_one[y] for y in lats
    ]
    last_next = [
        last_again[y]
        + first_last[y] * first_one[y]
        + last_last[y] * last_one[y]
        + (reciprocal[y] * last_one[y] if y < top else folded)
        for y in lats
    ]
    first_two, last_two = ends(first_next, last_next)

    def own(values):
        chosen = values[0]
        for y in range(1, devices_y):
            chosen = jnp.where(index_y == y, values[y], chosen)
        return jnp.sum(jnp.where(iota(chosen.shape, 0) == index_x, chosen, 0.0), axis=0, keepdims=True)

    current = (
        again[...]
        + merid[2] * own(first_one)
        + merid[3] * own(last_one)
        + merid[0] * own(first_two)
        + merid[1] * own(last_two)
    )
    current_out[...] = current
    rows = half_sums([zonal[0] * current, zonal[1] * current], levels)
    message[...] = jnp.broadcast_to(padded(rows, message.shape[2])[None], message.shape)


def zonal_again(factors_ref, zonal, current, out):
    out[...] = relax(current[...] * (zonal[2] > 0.0), load_factors(factors_ref), 1) * zonal[2]


def zonal_close(gathered, ring, zonal, direct, out):
    levels, height, width = out.shape
    lanes = levels * width
    index = lax.axis_index("lon")
    factors = [(ring[4 + 2 * k], ring[5 + 2 * k]) for k in range((ring.shape[0] - 4) // 2)]
    first, last = ring_ends(gathered[:, 0, :], gathered[:, 1, :], ring[0], ring[1], ring[2], factors, ring[3])
    result = zonal[4] * (
        direct[...]
        + zonal[0] * own_columns(first, index, height, levels, lanes)
        + zonal[1] * own_columns(last, index, height, levels, lanes)
    )
    for k in range(levels):
        out[k] = result[:, k * width : (k + 1) * width]


def run(body, shapes, *operands, scalars=()):
    vmem = pl.BlockSpec(memory_space=pltpu.VMEM)
    smem = pl.BlockSpec(memory_space=pltpu.SMEM)
    return pl.pallas_call(
        body,
        out_shape=[jax.ShapeDtypeStruct(shape, F32) for shape in shapes],
        in_specs=[smem if k in scalars else vmem for k in range(len(operands))],
        out_specs=[vmem] * len(shapes),
        name=body.__name__,
    )(*operands)


def steps(count):
    return (count - 1).bit_length()


def to_all(message, axis):
    return lax.all_to_all(message, axis, split_axis=0, concat_axis=0, tiled=True)


def local(field, gamma, kappa_zonal, kappa_merid, area, sea_mask, fold_pair):
    levels, height, width = field.shape
    lanes = levels * width
    devices_x, devices_y = lax.axis_size("lon"), lax.axis_size("lat")
    tile = (height, lanes)
    zonal_count, merid_count = 2 * steps(width - 2), 2 * steps(height - 2)

    message, zonal_factors, zonal = run(
        zonal_local,
        [(devices_x, 8, lanes), (zonal_count,) + tile, (5,) + tile],
        field, gamma, kappa_zonal, sea_mask,
    )
    gathered = to_all(message, "lon")
    direct, merid_factors, merid, merid_rows = run(
        merid_local,
        [tile, (merid_count,) + tile, (6,) + tile, (16, lanes)],
        zonal_factors, zonal, kappa_merid, area, sea_mask,
    )
    current, message, ring = run(
        zonal_join,
        [tile, (devices_x * devices_y, 16, lanes), (4 + 2 * steps(devices_x), devices_x, lanes)],
        gathered, zonal, direct, merid, merid_rows,
    )
    gathered = to_all(message, ("lon", "lat")).reshape(devices_x, devices_y, 16, lanes)
    (again,) = run(merid_twice, [tile], current, merid_factors, merid)
    current, message = run(
        merid_join, [tile, (devices_x, 8, lanes)], gathered, again, merid, zonal, fold_pair, scalars=(4,)
    )
    gathered = to_all(message, "lon")
    (direct,) = run(zonal_again, [tile], zonal_factors, zonal, current)
    (result,) = run(zonal_close, [(levels, height, width)], gathered, ring, zonal, direct)
    return result


def solution(mesh):
    blocks = P(None, "lat", "lon")
    return jax.shard_map(
        local,
        mesh=mesh,
        in_specs=(blocks, blocks, blocks, blocks, P("lat", "lon"), P("lat", "lon"), P("lon")),
        out_specs=blocks,
        check_vma=False,
    )
```

time: 189 us -> 48.2 us (0.26)
  blocking collectives: 91.9 us -> 0 us
  local copies, waits for them, and re-layouts: 24.2 us -> 1.93 us
  starting transfers between devices: 29.6 us -> 13.2 us
  Pallas kernels: 0 us -> 14.4 us
  other arithmetic: 14 us -> 0 us
  waiting for transfers between devices: 27.5 us -> 18.2 us
    all_gather x2 -> x0, blocking collectives: 61.6 us -> none  [fold_natural(): whole_row = lax.all_gather(top_cells, 'lon', axis=1, tiled=True)]
    all_to_all x4 -> x0, blocking collectives: 30.3 us -> none  [the longest x1 8.94 us: zonal_pass(): lax.all_to_all(current, 'lon', split_axis=1, concat_axis=2, tiled=True)]
    pallas_call x0 -> x7, Pallas kernels: none -> 14.4 us  [run(): pl.pallas_call(body, out_shape=[jax.ShapeDtypeStruct(shape, F32) for shap...]
    all_to_all x6 -> x3, waiting for transfers between devices: 27.5 us -> 18.2 us  [to_all(): lax.all_to_all(message, axis, split_axis=0, concat_axis=0, tiled=True)]
    all_to_all x6 -> x3, starting transfers between devices: 22.1 us -> 13.2 us  [to_all(): lax.all_to_all(message, axis, split_axis=0, concat_axis=0, tiled=True)]
    unnamed x35 -> x6, local copies, waits for them, and re-layouts: 10.7 us -> 1.93 us
    slice x121 -> x0, local copies, waits for them, and re-layouts: 7.61 us -> none  [the longest x83 5.08 us: slide(): return jnp.roll(values, offset, axis=-1)]
    ppermute x2 -> x0, starting transfers between devices: 7.44 us -> none  [the longest x1 6.03 us: passed_along(): return lax.ppermute(block, axis, route)]
  transfers between devices with their start and end apart: 8 -> 3, of which waited for: 6 -> 3; matrix products, arithmetic and copies ran while one was open for 2% -> 0% of each run, Pallas kernels for 0% -> 12%
where the time goes in v1:
time: 48.2 us; the launch traced here: 47.7 us
  waiting for transfers between devices  18.2 us (38%)
  Pallas kernels  14.4 us (30%)
  starting transfers between devices  13.2 us (27%)
  local copies, waits for them, and re-layouts  1.93 us (4%)
    all_to_all x3, waiting for transfers between devices, to_all(): lax.all_to_all(message, axis, split_axis=0, concat_axis=0, tiled=True)  18.2 us
    pallas_call x7, Pallas kernels, run(): pl.pallas_call(body, out_shape=[jax.ShapeDtypeStruct(shape, F32) for shap...  14.4 us
    all_to_all x3, starting transfers between devices, to_all(): lax.all_to_all(message, axis, split_axis=0, concat_axis=0, tiled=True)  13.2 us
    unnamed x6, local copies, waits for them, and re-layouts  1.93 us
  transfers between devices with their start and end apart: 3, of which 3 were waited for; matrix products, arithmetic and copies ran while one was open for 0% of the time, Pallas kernels for 12%

profile of v1, /device:TPU:0, one launch (start us, length us, event | category | flops | bytes accessed | tf_op | source)
XLA Modules:
  0.0 47.7 jit_solution(13062305697805148163)
XLA Ops:
  0.0 2.5 %zonal_local.1 = (f32[8,8,128]{2,1,0:T(8,128)}, f32[12,32,128]{2,1,0:T(8,128)}, f32[5,32,128]{2,1,0:T(8,128)}) custom-call(f32[2,32,64]{2,1,0:T(8,128)} %field.1, f32[2,32,64]{2,1,0:T(8,128)} %gamma.1, f32[2,32,64]{2,1,0:T(8,128)} %kappa.2, s32[32,64]{1,0:T(8,128)} %mask.3), custom_call_target="tpu_custom_call" | custom-call | tf_op jit(solution)/shard_map/zonal_local/pallas_call | solution.py:393
  2.5 7.3 %all-to-all-start = ((f32[8,8,128]{2,1,0:T(8,128)}), f32[8,8,128]{2,1,0:T(8,128)S(1)}, u32[]{:S(2)}, u32[]{:S(2)}) async-start(f32[8,8,128]{2,1,0:T(8,128)} %get-tuple-element.17), calls=%async_computation | async-start | bytes 65536 | tf_op jit(solution)/shard_map/all_to_all | solution.py:407
  9.7 2.1 %merid_local.1 = (f32[32,128]{1,0:T(8,128)}, f32[10,32,128]{2,1,0:T(8,128)}, f32[6,32,128]{2,1,0:T(8,128)}, f32[16,128]{1,0:T(8,128)}) custom-call(f32[12,32,128]{2,1,0:T(8,128)} %get-tuple-element.19.zonal_factors.factors_ref, f32[5,32,128]{2,1,0:T(8,128)} %get-tuple-element.18.zonal, f32[2,32,64]{2,1,0:T(8,128)} %kappa.3, f32[32,64]{1,0:T(8,128)} %area.1, ...), custom_call_target="tpu_custom_call" | custom-call | tf_op jit(solution)/shard_map/merid_local/pallas_call | solution.py:393
  11.8 4.6 %all-to-all-done.gathered = f32[8,8,128]{2,1,0:T(8,128)S(1)} async-done(((f32[8,8,128]{2,1,0:T(8,128)}), f32[8,8,128]{2,1,0:T(8,128)S(1)}, u32[]{:S(2)}, u32[]{:S(2)}) %all-to-all-start) | async-done | bytes 32800 | tf_op jit(solution)/shard_map/all_to_all | solution.py:407
  16.4 0.0 copy-start.2
  16.4 0.6 %copy-done.2 = f32[8,8,128]{2,1,0:T(8,128)} copy-done((f32[8,8,128]{2,1,0:T(8,128)}, f32[8,8,128]{2,1,0:T(8,128)S(1)}, u32[]{:S(2)}) %copy-start.2) | copy-done | bytes 32792
  17.0 1.8 %zonal_join.1 = (f32[32,128]{1,0:T(8,128)}, f32[32,16,128]{2,1,0:T(8,128)}, f32[10,8,128]{2,1,0:T(8,128)}) custom-call(f32[8,8,128]{2,1,0:T(8,128)} %copy-done.2, f32[5,32,128]{2,1,0:T(8,128)} %get-tuple-element.18.zonal, f32[32,128]{1,0:T(8,128)} %get-tuple-element.20.direct, f32[6,32,128]{2,1,0:T(8,128)} %get-tuple-element.21.merid, ...), custom_call_target="tpu_custom_call" | custom-call | tf_op jit(solution)/shard_map/zonal_join/pallas_call | solution.py:393
  18.9 2.6 %all-to-all-start.1 = ((f32[32,16,128]{2,1,0:T(8,128)}), f32[32,16,128]{2,1,0:T(8,128)S(1)}, u32[]{:S(2)}, u32[]{:S(2)}) async-start(f32[32,16,128]{2,1,0:T(8,128)} %get-tuple-element.23), calls=%async_computation.1 | async-start | bytes 524288 | tf_op jit(solution)/shard_map/all_to_all | solution.py:407
  21.4 1.6 %merid_twice.1.again = f32[32,128]{1,0:T(8,128)} custom-call(f32[32,128]{1,0:T(8,128)} %get-tuple-element.24.current, f32[10,32,128]{2,1,0:T(8,128)} %get-tuple-element.25.factors_ref, f32[6,32,128]{2,1,0:T(8,128)} %get-tuple-element.21.merid), custom_call_target="tpu_custom_call" | custom-call | tf_op jit(solution)/shard_map/merid_twice/pallas_call | solution.py:393
  23.1 9.0 %all-to-all-done.1 = f32[32,16,128]{2,1,0:T(8,128)S(1)} async-done(((f32[32,16,128]{2,1,0:T(8,128)}), f32[32,16,128]{2,1,0:T(8,128)S(1)}, u32[]{:S(2)}, u32[]{:S(2)}) %all-to-all-start.1) | async-done | bytes 262176 | tf_op jit(solution)/shard_map/all_to_all | solution.py:407
  32.0 0.0 copy-start
  32.0 0.7 %copy-done = f32[32,16,128]{2,1,0:T(8,128)} copy-done((f32[32,16,128]{2,1,0:T(8,128)}, f32[32,16,128]{2,1,0:T(8,128)S(1)}, u32[]{:S(2)}) %copy-start) | copy-done | bytes 262168
  32.7 2.6 %merid_join.1 = (f32[32,128]{1,0:T(8,128)}, f32[8,8,128]{2,1,0:T(8,128)}) custom-call(f32[8,4,16,128]{3,2,1,0:T(8,128)} %bitcast.1, f32[32,128]{1,0:T(8,128)} %merid_twice.1.again, f32[6,32,128]{2,1,0:T(8,128)} %get-tuple-element.21.merid, f32[5,32,128]{2,1,0:T(8,128)} %get-tuple-element.18.zonal, s32[64]{0:T(128)} %pairing.1), custom_call_target="tpu_custom_call" | custom-call | tf_op jit(solution)/shard_map/merid_join/pallas_call | solution.py:393
  35.4 3.3 %all-to-all-start.2 = ((f32[8,8,128]{2,1,0:T(8,128)}), f32[8,8,128]{2,1,0:T(8,128)S(1)}, u32[]{:S(2)}, u32[]{:S(2)}) async-start(f32[8,8,128]{2,1,0:T(8,128)} %get-tuple-element.26), calls=%async_computation.2 | async-start | bytes 65536 | tf_op jit(solution)/shard_map/all_to_all | solution.py:407
  38.7 2.0 %zonal_again.1.direct = f32[32,128]{1,0:T(8,128)} custom-call(f32[12,32,128]{2,1,0:T(8,128)} %get-tuple-element.19.zonal_factors.factors_ref, f32[5,32,128]{2,1,0:T(8,128)} %get-tuple-element.18.zonal, f32[32,128]{1,0:T(8,128)} %get-tuple-element.28.current), custom_call_target="tpu_custom_call" | custom-call | tf_op jit(solution)/shard_map/zonal_again/pallas_call | solution.py:393
  40.7 4.6 %all-to-all-done.2.gathered = f32[8,8,128]{2,1,0:T(8,128)S(1)} async-done(((f32[8,8,128]{2,1,0:T(8,128)}), f32[8,8,128]{2,1,0:T(8,128)S(1)}, u32[]{:S(2)}, u32[]{:S(2)}) %all-to-all-start.2) | async-done | bytes 32800 | tf_op jit(solution)/shard_map/all_to_all | solution.py:407
  45.3 0.0 copy-start.1
  45.3 0.6 %copy-done.1 = f32[8,8,128]{2,1,0:T(8,128)} copy-done((f32[8,8,128]{2,1,0:T(8,128)}, f32[8,8,128]{2,1,0:T(8,128)S(1)}, u32[]{:S(2)}) %copy-start.1) | copy-done | bytes 32792
  45.9 1.7 %zonal_close.1 = f32[2,32,64]{2,1,0:T(8,128)} custom-call(f32[8,8,128]{2,1,0:T(8,128)} %copy-done.1, f32[10,8,128]{2,1,0:T(8,128)} %get-tuple-element.27.ring, f32[5,32,128]{2,1,0:T(8,128)} %get-tuple-element.18.zonal, f32[32,128]{1,0:T(8,128)} %zonal_again.1.direct), custom_call_target="tpu_custom_call" | custom-call | tf_op jit(solution)/shard_map/zonal_close/pallas_call | solution.py:393
Async XLA Ops:
  2.5 13.9 %all-to-all-start = ((f32[8,8,128]{2,1,0:T(8,128)}), f32[8,8,128]{2,1,0:T(8,128)S(1)}, u32[]{:S(2)}, u32[]{:S(2)}) async-start(f32[8,8,128]{2,1,0:T(8,128)} %get-tuple-element.17), calls=%async_computation | async-start | bytes 65536 | tf_op jit(solution)/shard_map/all_to_all | solution.py:407
  16.4 0.6 %copy-start.2 = (f32[8,8,128]{2,1,0:T(8,128)}, f32[8,8,128]{2,1,0:T(8,128)S(1)}, u32[]{:S(2)}) copy-start(f32[8,8,128]{2,1,0:T(8,128)S(1)} %all-to-all-done.gathered) | copy-start | bytes 98308
  18.9 13.2 %all-to-all-start.1 = ((f32[32,16,128]{2,1,0:T(8,128)}), f32[32,16,128]{2,1,0:T(8,128)S(1)}, u32[]{:S(2)}, u32[]{:S(2)}) async-start(f32[32,16,128]{2,1,0:T(8,128)} %get-tuple-element.23), calls=%async_computation.1 | async-start | bytes 524288 | tf_op jit(solution)/shard_map/all_to_all | solution.py:407
  32.0 0.7 %copy-start = (f32[32,16,128]{2,1,0:T(8,128)}, f32[32,16,128]{2,1,0:T(8,128)S(1)}, u32[]{:S(2)}) copy-start(f32[32,16,128]{2,1,0:T(8,128)S(1)} %all-to-all-done.1) | copy-start | bytes 786436
  35.4 10.0 %all-to-all-start.2 = ((f32[8,8,128]{2,1,0:T(8,128)}), f32[8,8,128]{2,1,0:T(8,128)S(1)}, u32[]{:S(2)}, u32[]{:S(2)}) async-start(f32[8,8,128]{2,1,0:T(8,128)} %get-tuple-element.26), calls=%async_computation.2 | async-start | bytes 65536 | tf_op jit(solution)/shard_map/all_to_all | solution.py:407
  45.3 0.6 %copy-start.1 = (f32[8,8,128]{2,1,0:T(8,128)}, f32[8,8,128]{2,1,0:T(8,128)S(1)}, u32[]{:S(2)}) copy-start(f32[8,8,128]{2,1,0:T(8,128)S(1)} %all-to-all-done.2.gathered) | copy-start | bytes 98308

commit v2 on v0

v2 whole, which is shorter than its diff:
```python
import functools

import jax
import jax.numpy as jnp
from jax import lax
from jax.experimental import pallas as pl
from jax.experimental.pallas import tpu as pltpu
from jax.sharding import PartitionSpec as P


F32 = jnp.float32
EXACT = lax.Precision.HIGHEST


def moved(values, distance, axis):
    return pltpu.roll(values, distance % values.shape[axis], axis)


def iota(shape, axis):
    return lax.broadcasted_iota(jnp.int32, shape, axis)


def spread(values, up, down, stride, axis):
    return values + moved(up * values, stride, axis) + moved(down * values, -stride, axis)


def condense(left, right, totals, count, axis):
    factors = []
    stride = 1
    while stride < count:
        pull = 1.0 / (totals[0] + left + right)
        up, down = right * pull, left * pull
        link = left * up
        factors.append((up, down))
        totals = [spread(t, up, down, stride, axis) for t in totals]
        left, right = moved(link, stride, axis), moved(link, -stride, axis)
        stride *= 2
    return factors, totals


def relax(values, factors, axis):
    stride = 1
    for up, down in factors:
        values = spread(values, up, down, stride, axis)
        stride *= 2
    return values


def load_factors(ref):
    return [(ref[2 * k], ref[2 * k + 1]) for k in range(ref.shape[0] // 2)]


def store_factors(ref, factors):
    for k, (up, down) in enumerate(factors):
        ref[2 * k] = up
        ref[2 * k + 1] = down


def beside(ref):
    return jnp.concatenate([ref[k] for k in range(ref.shape[0])], axis=-1)


def chain(faces, place, length, axis):
    inner = (place >= 1) & (place <= length - 3)
    right = jnp.where(inner, faces, 0.0)
    left = moved(right, 1, axis)
    to_first = jnp.where(place == 1, moved(faces, 1, axis), 0.0)
    to_last = jnp.where(place == length - 2, faces, 0.0)
    return left, right, to_first, to_last


def half_sums(arrays, levels):
    wide = jnp.concatenate(arrays, axis=1)
    lanes = arrays[0].shape[1]
    width = lanes // levels
    shape = (8 * levels, wide.shape[1])
    row, col = iota(shape, 0), iota(shape, 1)
    pick = ((col // lanes == row % 8) & (col % lanes // width == row // 8)).astype(F32)
    sums = lax.dot_general(pick, wide, (((1,), (1,)), ((), ())), precision=EXACT, preferred_element_type=F32)
    return jnp.concatenate([sums[8 * k : 8 * k + 8] for k in range(levels)], axis=1)


def padded(rows, lanes):
    return jnp.concatenate([rows, jnp.zeros((rows.shape[0], lanes - rows.shape[1]), F32)], axis=1)


def fetch(sources, buffers, semaphores):
    copies = [
        pltpu.make_async_copy(source, buffer, semaphores.at[k])
        for k, (source, buffer) in enumerate(zip(sources, buffers))
    ]
    for copy in copies:
        copy.start()
    for copy in copies:
        copy.wait()


def block_local(*refs):
    sources, (message, payload, factors_out, keep), buffers, semaphores = refs[:6], refs[6:10], refs[10:16], refs[16]
    fetch(sources, buffers, semaphores)
    field, gamma, kappa_zonal, kappa_merid, area, mask = buffers
    levels, height, width = field.shape
    lanes = levels * width
    ocean_one = mask[...].astype(F32)
    ocean = jnp.concatenate([ocean_one] * levels, axis=1)
    place = iota((height, lanes), 1) % width
    scaled = beside(gamma) * ocean
    source = scaled * beside(field)
    open_face = beside(kappa_zonal) * ocean
    faces = open_face * moved(ocean, -1, 1)
    left, right, to_first, to_last = chain(faces, place, width, 1)
    inner = (place >= 1) & (place <= width - 2)
    factors, (ground, first, last, direct) = condense(
        left,
        right,
        [1.0 + to_first + to_last, to_first, to_last, jnp.where(inner, source, 0.0)],
        width - 2,
        1,
    )
    inverse = jnp.where(inner, 1.0 / ground, 0.0)
    first = first * inverse
    last = last * inverse
    edge = to_first * last
    first = jnp.where(place == 0, 1.0, first)
    last = jnp.where(place == width - 1, 1.0, last)
    rows = half_sums(
        [
            first * source,
            last * source,
            first,
            last,
            edge,
            jnp.where(place == width - 1, open_face, 0.0),
            jnp.where(place == 0, ocean, 0.0),
        ],
        levels,
    )
    message[...] = jnp.broadcast_to(jnp.concatenate([rows[:4], rows[4:]], axis=1)[None], message.shape)
    payload[0] = direct * inverse
    payload[1] = first
    payload[2] = last
    payload[3] = beside(kappa_merid) * ocean
    payload[4] = jnp.concatenate([1.0 / area[...], ocean_one], axis=1)
    store_factors(factors_out, factors)
    keep[0] = first
    keep[1] = last
    keep[2] = inverse
    keep[3] = scaled


def ring_setup(first_ground, last_ground, edge, open_face, ocean):
    face = open_face * moved(ocean, -1, 0)
    last_pull = 1.0 / (last_ground + edge + face)
    edge_pull, face_pull = edge * last_pull, face * last_pull
    ground = first_ground + edge_pull * last_ground + moved(face_pull * last_ground, 1, 0)
    link = edge * face_pull
    factors, (ground,) = condense(moved(link, 1, 0), link, [ground], edge.shape[0], 0)
    return edge_pull, face_pull, last_pull, factors, 1.0 / ground


def ring_ends(first_source, last_source, edge_pull, face_pull, last_pull, factors, inverse):
    values = first_source + edge_pull * last_source + moved(face_pull * last_source, 1, 0)
    first = relax(values, factors, 0) * inverse
    last = last_pull * last_source + edge_pull * first + face_pull * moved(first, -1, 0)
    return first, last


def own_row(values, index):
    return jnp.sum(jnp.where(iota(values.shape, 0) == index, values, 0.0), axis=0, keepdims=True)


def columns(own, block, height, levels, lanes):
    width = lanes // levels
    row, col = iota((height, lanes), 0), iota((height, lanes), 1)
    result = None
    for k in range(levels):
        base = (block * levels + k) * height
        group = own[:, base // lanes * lanes : base // lanes * lanes + lanes]
        column = jnp.sum(jnp.where(col == row + base % lanes, group, 0.0), axis=1, keepdims=True)
        result = jnp.broadcast_to(column, (height, lanes)) if k == 0 else jnp.where(col >= k * width, column, result)
    return result


def column_join(gathered, payload, keep, kept, message):
    levels = 2
    devices_y, _, height, lanes = payload.shape
    lines = levels * height
    index_x, index_y = lax.axis_index("lon"), lax.axis_index("lat")
    half = lanes // 2

    def quantity(k):
        lane = k // 4 * half
        return jnp.concatenate(
            [gathered[:, y, k % 4, :][:, lane : lane + lines] for y in range(devices_y)], axis=1
        )

    first_source, last_source, first_ground, last_ground, edge, open_face, ocean = [quantity(k) for k in range(7)]
    ring = ring_setup(first_ground, last_ground, edge, open_face, ocean)
    first_ends, last_ends = ring_ends(first_source, last_source, *ring)
    first_ends, last_ends = own_row(first_ends, index_x), own_row(last_ends, index_x)
    current = jnp.concatenate(
        [
            payload[y, 0]
            + payload[y, 1] * columns(first_ends, y, height, levels, lanes)
            + payload[y, 2] * columns(last_ends, y, height, levels, lanes)
            for y in range(devices_y)
        ],
        axis=0,
    )
    open_face = jnp.concatenate([payload[y, 3] for y in range(devices_y)], axis=0)
    packed = jnp.concatenate([payload[y, 4] for y in range(devices_y)], axis=0)
    reciprocal = jnp.concatenate([packed[:, :half]] * levels, axis=1)
    ocean = jnp.concatenate([packed[:, half:]] * levels, axis=1)
    count = devices_y * height
    row = iota((count, lanes), 0)
    top = row == count - 1
    faces = jnp.where(top, 0.0, open_face * moved(ocean, -1, 0))
    factors, (ground, current, reach) = condense(
        moved(faces, 1, 0), faces, [jnp.ones_like(faces), current, top.astype(F32)], count, 0
    )
    inverse = 1.0 / ground
    current = current * inverse
    reach = reach * inverse
    again = relax(jnp.where(top, 0.0, current * reciprocal), factors, 0) * inverse

    def own_block(values):
        chosen = values[:height]
        for y in range(1, devices_y):
            chosen = jnp.where(index_y == y, values[y * height : (y + 1) * height], chosen)
        return chosen

    again, reach = own_block(again), own_block(reach)
    kept[0] = again
    kept[1] = reach
    rows = half_sums([keep[0] * again, keep[1] * again], levels)
    whole = jnp.concatenate(
        [
            keep[0] * reach,
            keep[1] * reach,
            jnp.concatenate([rows[:1], rows[1:2]], axis=1),
            current[count - 1 :],
            reciprocal[count - 1 :],
            jnp.zeros((5, lanes), F32),
        ],
        axis=0,
    )
    message[...] = jnp.broadcast_to(whole[None], message.shape)


def mirrored(values, pivot, width):
    count, lanes = values.shape
    devices = count // 2
    pivot_block, pivot_place = pivot // width, pivot % width
    source, target = iota((lanes, lanes), 0), iota((lanes, lanes), 1)
    reach = pivot_place - target % width
    same = source // width == target // width
    goal, origin = iota((count, count), 0), iota((count, count), 1)
    result = 0.0
    for extra in range(2):
        lane_pick = (same & (source % width == reach + extra * width)).astype(F32)
        turned = lax.dot(values, lane_pick, precision=EXACT, preferred_element_type=F32)
        wanted = (pivot_block - goal % devices - extra + 2 * devices) % devices
        block_pick = ((goal // devices == origin // devices) & (origin % devices == wanted)).astype(F32)
        result = result + lax.dot(block_pick, turned, precision=EXACT, preferred_element_type=F32)
    return result


def zonal_close(gathered, ring_rows, kept, factors_ref, keep, pairing, out):
    levels, height, width = out.shape
    lanes = levels * width
    lines = levels * height
    half = lanes // 2
    devices = gathered.shape[0]
    index_x, index_y = lax.axis_index("lon"), lax.axis_index("lat")
    mine = ring_rows[:, pl.ds(index_y, 1), :, :].reshape(devices, 4, lanes)
    ring = ring_setup(
        mine[:, 2, :lines],
        mine[:, 3, :lines],
        mine[:, 0, half : half + lines],
        mine[:, 1, half : half + lines],
        mine[:, 2, half : half + lines],
    )
    top, reciprocal = gathered[:, lines + 1, :], gathered[:, lines + 2, :]
    pivot = (pairing[0] + index_x * width) % (devices * width)
    across = mirrored(jnp.concatenate([top, reciprocal], axis=0), pivot, width)
    folded = 0.25 * (top + across[:devices]) * (reciprocal + across[devices:])
    tiled = jnp.concatenate([folded] * devices, axis=1)
    row, col = iota(tiled.shape, 0), iota(tiled.shape, 1)
    picks = jnp.concatenate(
        [jnp.where((col // lanes == row) & (col % lanes // width == k), tiled, 0.0) for k in range(levels)], axis=0
    )
    reach = jnp.concatenate([gathered[b, : 2 * height, :] for b in range(devices)], axis=1)
    change = lax.dot_general(
        picks, reach, (((1,), (1,)), ((), ())), precision=EXACT, preferred_element_type=F32
    )
    change = [change[k * devices : (k + 1) * devices] for k in range(levels)]
    first_source = gathered[:, lines, :][:, :lines] + jnp.concatenate([c[:, :height] for c in change], axis=1)
    last_source = gathered[:, lines, :][:, half : half + lines] + jnp.concatenate(
        [c[:, height:] for c in change], axis=1
    )
    first_ends, last_ends = ring_ends(first_source, last_source, *ring)
    current = kept[0] + kept[1] * own_row(folded, index_x)
    inner = keep[2] > 0.0
    direct = relax(jnp.where(inner, current, 0.0), load_factors(factors_ref), 1) * keep[2]

    def ends(values):
        own = own_row(values, index_x)
        return columns(jnp.concatenate([own, own], axis=1)[:, :lanes], 0, height, levels, lanes)

    result = keep[3] * (direct + keep[0] * ends(first_ends) + keep[1] * ends(last_ends))
    for k in range(levels):
        out[k] = result[:, k * width : (k + 1) * width]


def run(body, shapes, *operands, scalars=(), outside=(), scratch=(), limit=8 << 20):
    vmem = pl.BlockSpec(memory_space=pltpu.VMEM)
    smem = pl.BlockSpec(memory_space=pltpu.SMEM)
    hbm = pl.BlockSpec(memory_space=pltpu.HBM)
    return pl.pallas_call(
        body,
        out_shape=[jax.ShapeDtypeStruct(shape, F32) for shape in shapes],
        in_specs=[smem if k in scalars else hbm if k in outside else vmem for k in range(len(operands))],
        out_specs=[vmem] * len(shapes),
        scratch_shapes=scratch,
        compiler_params=pltpu.CompilerParams(vmem_limit_bytes=limit),
        name=body.__name__,
    )(*operands)


def local(field, gamma, kappa_zonal, kappa_merid, area, sea_mask, fold_pair):
    levels, height, width = field.shape
    lanes = levels * width
    devices_x, devices_y = lax.axis_size("lon"), lax.axis_size("lat")
    tile = (height, lanes)
    count = 2 * (width - 3).bit_length()
    operands = (field, gamma, kappa_zonal, kappa_merid, area, sea_mask)
    scratch = [pltpu.VMEM(x.shape, x.dtype) for x in operands] + [pltpu.SemaphoreType.DMA((len(operands),))]
    message, payload, factors, keep = run(
        block_local,
        [(devices_x * devices_y, 4, lanes), (5,) + tile, (count,) + tile, (4,) + tile],
        *operands,
        outside=range(len(operands)),
        scratch=scratch,
        limit=None,
    )
    ring_rows = lax.all_to_all(message, ("lon", "lat"), split_axis=0, concat_axis=0, tiled=True)
    ring_rows = ring_rows.reshape(devices_x, devices_y, 4, lanes)
    payload = lax.all_gather(payload, "lat", axis=0, tiled=False)
    kept, message = run(
        column_join, [(2,) + tile, (devices_x, 2 * height + 8, lanes)], ring_rows, payload, keep
    )
    gathered = lax.all_to_all(message, "lon", split_axis=0, concat_axis=0, tiled=True)
    (result,) = run(
        zonal_close, [(levels, height, width)], gathered, ring_rows, kept, factors, keep, fold_pair, scalars=(5,)
    )
    return result


def solution(mesh):
    blocks = P(None, "lat", "lon")
    return jax.shard_map(
        local,
        mesh=mesh,
        in_specs=(blocks, blocks, blocks, blocks, P("lat", "lon"), P("lat", "lon"), P("lon")),
        out_specs=blocks,
        check_vma=False,
    )
```

time: 189 us -> 37.5 us (0.20)
  blocking collectives: 91.9 us -> 22.4 us
  waiting for transfers between devices: 27.5 us -> 0.51 us
  local copies, waits for them, and re-layouts: 24.2 us -> 0.66 us
  starting transfers between devices: 29.6 us -> 7.3 us
  other arithmetic: 14 us -> 0 us
  Pallas kernels: 0 us -> 6.23 us
    all_gather x2 -> x1, blocking collectives: 61.6 us -> 6.87 us  [local(): payload = lax.all_gather(payload, 'lat', axis=0, tiled=False)]
    all_to_all x6 -> x1, waiting for transfers between devices: 27.5 us -> 0.51 us  [local(): lax.all_to_all(message, ('lon', 'lat'), split_axis=0, concat_axis=0, tile...]
    all_to_all x6 -> x1, starting transfers between devices: 22.1 us -> 7.3 us  [local(): lax.all_to_all(message, ('lon', 'lat'), split_axis=0, concat_axis=0, tile...]
    all_to_all x4 -> x1, blocking collectives: 30.3 us -> 15.5 us  [local(): lax.all_to_all(message, 'lon', split_axis=0, concat_axis=0, tiled=True)]
    unnamed x35 -> x8, local copies, waits for them, and re-layouts: 10.7 us -> 0.66 us
    slice x121 -> x0, local copies, waits for them, and re-layouts: 7.61 us -> none  [the longest x83 5.08 us: slide(): return jnp.roll(values, offset, axis=-1)]
    ppermute x2 -> x0, starting transfers between devices: 7.44 us -> none  [the longest x1 6.03 us: passed_along(): return lax.ppermute(block, axis, route)]
    all_to_all x10 -> x0, other arithmetic: 7.27 us -> none  [the longest x2 1.46 us: merid_open(): lax.all_to_all(to_columns(current, lanes), 'lat', split_axis=0, concat_ax...]
  transfers between devices with their start and end apart: 8 -> 1, of which waited for: 6 -> 1; matrix products, arithmetic and copies ran while one was open for 2% -> 0% of each run, Pallas kernels for 0% -> 0%
where the time goes in v2:
time: 37.5 us; the launch traced here: 37.1 us
  blocking collectives  22.4 us (60%)
  starting transfers between devices  7.3 us (19%)
  Pallas kernels  6.23 us (17%)
  local copies, waits for them, and re-layouts  0.66 us (2%)
  waiting for transfers between devices  0.51 us (1%)
    all_to_all x1, blocking collectives, local(): lax.all_to_all(message, 'lon', split_axis=0, concat_axis=0, tiled=True)  15.5 us
    all_to_all x1, starting transfers between devices, local(): lax.all_to_all(message, ('lon', 'lat'), split_axis=0, concat_axis=0, tile...  7.3 us
    all_gather x1, blocking collectives, local(): payload = lax.all_gather(payload, 'lat', axis=0, tiled=False)  6.87 us
    pallas_call x3, Pallas kernels, run(): pl.pallas_call(body, out_shape=[jax.ShapeDtypeStruct(shape, F32) for shap...  6.23 us
  transfers between devices with their start and end apart: 1, of which 1 were waited for; matrix products, arithmetic and copies ran while one was open for 0% of the time, Pallas kernels for 0%

profile of v2, /device:TPU:0, one launch (start us, length us, event | category | flops | bytes accessed | tf_op | source)
XLA Modules:
  0.0 37.1 jit_solution(16053782904812782142)
XLA Ops:
  0.0 2.8 %block_local.1 = (f32[32,4,128]{2,1,0:T(4,128)}, f32[5,32,128]{2,1,0:T(8,128)}, f32[12,32,128]{2,1,0:T(8,128)}, f32[4,32,128]{2,1,0:T(8,128)}) custom-call(f32[2,32,64]{2,1,0:T(8,128)} %refs_0_.1, f32[2,32,64]{2,1,0:T(8,128)} %refs_1_.1, f32[2,32,64]{2,1,0:T(8,128)} %refs_2_.1, f32[2,32,64]{2,1,0:T(8,128)} %refs_3_.1, f32[32,64]{1,0:T(8,128)} %refs_4_.1, ...), custom_call_target="tpu_custom_call" | custom-call | tf_op jit(solution)/shard_map/block_local/pallas_call | solution.py:319
  2.8 0.0 copy-start.3
  2.8 7.3 %all-to-all-start = ((f32[32,4,128]{2,1,0:T(4,128)}), f32[32,4,128]{2,1,0:T(4,128)S(1)}, u32[]{:S(2)}, u32[]{:S(2)}) async-start(f32[32,4,128]{2,1,0:T(4,128)} %get-tuple-element.11), calls=%async_computation | async-start | bytes 131072 | tf_op jit(solution)/shard_map/all_to_all | solution.py:346
  10.1 0.0 copy-done.3
  10.2 0.0 copy-start
  10.2 6.9 %all-gather = f32[20,32,128]{2,1,0:T(8,128)S(1)} all-gather(f32[5,32,128]{2,1,0:T(8,128)S(1)} %copy-done.3), channel_id=2, replica_groups=mesh['lon'=8,'lat'=4] {'lat'}, dimensions={0}, use_global_device_ids=true | all-gather | bytes 409600 | tf_op jit(solution)/shard_map/all_gather | solution.py:348
  17.0 0.5 %all-to-all-done = f32[32,4,128]{2,1,0:T(4,128)S(1)} async-done(((f32[32,4,128]{2,1,0:T(4,128)}), f32[32,4,128]{2,1,0:T(4,128)S(1)}, u32[]{:S(2)}, u32[]{:S(2)}) %all-to-all-start) | async-done | bytes 65568 | tf_op jit(solution)/shard_map/all_to_all | solution.py:346
  17.6 0.0 copy-done
  17.6 0.9 %column_join.1 = (f32[2,32,128]{2,1,0:T(8,128)S(1)}, f32[8,72,128]{2,1,0:T(8,128)S(1)}) custom-call(f32[8,4,4,128]{3,2,1,0:T(4,128)S(1)} %bitcast.3, f32[4,5,32,128]{3,2,1,0:T(8,128)S(1)} %bitcast.2, f32[4,32,128]{2,1,0:T(8,128)S(1)} %copy-done), custom_call_target="tpu_custom_call" | custom-call | tf_op jit(solution)/shard_map/column_join/pallas_call | solution.py:319
  18.5 0.0 copy-start.1
  18.5 15.5 %all_to_all.10.gathered = f32[8,72,128]{2,1,0:T(8,128)S(1)} all-to-all(f32[8,72,128]{2,1,0:T(8,128)S(1)} %get-tuple-element.14), channel_id=1, replica_groups=mesh['lon'=8,'lat'=4] {'lon'}, dimensions={0} | all-to-all | bytes 589824 | tf_op jit(solution)/shard_map/all_to_all | solution.py:352
  34.0 0.0 copy-start.2
  34.0 0.0 copy-done.1
  34.0 0.7 %copy-done.2 = s32[64]{0:T(128)S(1)} copy-done((s32[64]{0:T(128)S(1)}, s32[64]{0:T(128)}, u32[]{:S(2)}) %copy-start.2) | copy-done | bytes 280
  34.7 2.5 %zonal_close.1 = f32[2,32,64]{2,1,0:T(8,128)} custom-call(f32[8,72,128]{2,1,0:T(8,128)S(1)} %all_to_all.10.gathered, f32[8,4,4,128]{3,2,1,0:T(4,128)S(1)} %bitcast.4, f32[2,32,128]{2,1,0:T(8,128)S(1)} %get-tuple-element.15.kept, f32[12,32,128]{2,1,0:T(8,128)S(1)} %copy-done.1, f32[4,32,128]{2,1,0:T(8,128)S(1)} %copy-done, s32[64]{0:T(128)S(1)} %copy-done.2), custom_call_target="tpu_custom_call" | custom-call | tf_op jit(solution)/shard_map/zonal_close/pallas_call | solution.py:319
Async XLA Ops:
  2.8 7.3 %copy-start.3 = (f32[5,32,128]{2,1,0:T(8,128)S(1)}, f32[5,32,128]{2,1,0:T(8,128)}, u32[]{:S(2)}) copy-start(f32[5,32,128]{2,1,0:T(8,128)} %get-tuple-element.12) | copy-start | bytes 245764
  2.8 14.7 %all-to-all-start = ((f32[32,4,128]{2,1,0:T(4,128)}), f32[32,4,128]{2,1,0:T(4,128)S(1)}, u32[]{:S(2)}, u32[]{:S(2)}) async-start(f32[32,4,128]{2,1,0:T(4,128)} %get-tuple-element.11), calls=%async_computation | async-start | bytes 131072 | tf_op jit(solution)/shard_map/all_to_all | solution.py:346
  10.2 7.4 %copy-start = (f32[4,32,128]{2,1,0:T(8,128)S(1)}, f32[4,32,128]{2,1,0:T(8,128)}, u32[]{:S(2)}) copy-start(f32[4,32,128]{2,1,0:T(8,128)} %get-tuple-element.13.keep) | copy-start | bytes 196612
  18.5 15.5 %copy-start.1 = (f32[12,32,128]{2,1,0:T(8,128)S(1)}, f32[12,32,128]{2,1,0:T(8,128)}, u32[]{:S(2)}) copy-start(f32[12,32,128]{2,1,0:T(8,128)} %get-tuple-element.16.factors_ref) | copy-start | bytes 589828
  34.0 0.7 %copy-start.2 = (s32[64]{0:T(128)S(1)}, s32[64]{0:T(128)}, u32[]{:S(2)}) copy-start(s32[64]{0:T(128)} %pairing.1) | copy-start | bytes 772

commit v3 on v2

--- a/solution.py
+++ b/solution.py
@@ -96,9 +96,11 @@
 
 
 def block_local(*refs):
-    sources, (message, payload, factors_out, keep), buffers, semaphores = refs[:6], refs[6:10], refs[10:16], refs[16]
+    sources, (message, payload, factors_out, keep, turn), buffers, semaphores = (
+        refs[:7], refs[7:12], refs[12:19], refs[19]
+    )
     fetch(sources, buffers, semaphores)
-    field, gamma, kappa_zonal, kappa_merid, area, mask = buffers
+    field, gamma, kappa_zonal, kappa_merid, area, mask, pairing = buffers
     levels, height, width = field.shape
     lanes = levels * width
     ocean_one = mask[...].astype(F32)
@@ -146,6 +148,7 @@
     keep[1] = last
     keep[2] = inverse
     keep[3] = scaled
+    turn[...] = jnp.full(turn.shape, pairing[0] + lax.axis_index("lon") * width, jnp.int32)
 
 
 def ring_setup(first_ground, last_ground, edge, open_face, ocean):
@@ -247,25 +250,24 @@
     message[...] = jnp.broadcast_to(whole[None], message.shape)
 
 
-def mirrored(values, pivot, width):
-    count, lanes = values.shape
-    devices = count // 2
-    pivot_block, pivot_place = pivot // width, pivot % width
-    source, target = iota((lanes, lanes), 0), iota((lanes, lanes), 1)
-    reach = pivot_place - target % width
-    same = source // width == target // width
-    goal, origin = iota((count, count), 0), iota((count, count), 1)
-    result = 0.0
-    for extra in range(2):
-        lane_pick = (same & (source % width == reach + extra * width)).astype(F32)
-        turned = lax.dot(values, lane_pick, precision=EXACT, preferred_element_type=F32)
-        wanted = (pivot_block - goal % devices - extra + 2 * devices) % devices
-        block_pick = ((goal // devices == origin // devices) & (origin % devices == wanted)).astype(F32)
-        result = result + lax.dot(block_pick, turned, precision=EXACT, preferred_element_type=F32)
-    return result
-
-
-def zonal_close(gathered, ring_rows, kept, factors_ref, keep, pairing, out):
+def mirrored(rows, pivot, width):
+    devices, lanes = rows[0].shape
+    block, lane = iota((devices, lanes), 0), iota((devices, lanes), 1)
+    place = lane % width
+    pivot_block, pivot_place = pivot // width % devices, pivot % width
+    reach = lane - place + (pivot_place - place + width) % width
+    wanted = (pivot_block - block - (place > pivot_place).astype(jnp.int32) + 2 * devices) % devices
+    results = []
+    for values in rows:
+        turned = jnp.take_along_axis(values, reach, axis=1)
+        result = turned
+        for b in range(devices):
+            result = jnp.where(wanted == b, turned[b : b + 1], result)
+        results.append(result)
+    return results
+
+
+def zonal_close(gathered, ring_rows, kept, factors_ref, keep, turn, out):
     levels, height, width = out.shape
     lanes = levels * width
     lines = levels * height
@@ -281,9 +283,8 @@
         mine[:, 2, half : half + lines],
     )
     top, reciprocal = gathered[:, lines + 1, :], gathered[:, lines + 2, :]
-    pivot = (pairing[0] + index_x * width) % (devices * width)
-    across = mirrored(jnp.concatenate([top, reciprocal], axis=0), pivot, width)
-    folded = 0.25 * (top + across[:devices]) * (reciprocal + across[devices:])
+    top_across, reciprocal_across = mirrored([top, reciprocal], turn[:devices], width)
+    folded = 0.25 * (top + top_across) * (reciprocal + reciprocal_across)
     tiled = jnp.concatenate([folded] * devices, axis=1)
     row, col = iota(tiled.shape, 0), iota(tiled.shape, 1)
     picks = jnp.concatenate(
@@ -312,46 +313,58 @@
         out[k] = result[:, k * width : (k + 1) * width]
 
 
-def run(body, shapes, *operands, scalars=(), outside=(), scratch=(), limit=8 << 20):
+def run(body, shapes, *operands, outside=False, scratch=()):
     vmem = pl.BlockSpec(memory_space=pltpu.VMEM)
-    smem = pl.BlockSpec(memory_space=pltpu.SMEM)
     hbm = pl.BlockSpec(memory_space=pltpu.HBM)
+    if outside:
+        operands = [pltpu.with_memory_space_constraint(x, pltpu.HBM) for x in operands]
     return pl.pallas_call(
         body,
-        out_shape=[jax.ShapeDtypeStruct(shape, F32) for shape in shapes],
-        in_specs=[smem if k in scalars else hbm if k in outside else vmem for k in range(len(operands))],
+        out_shape=shapes,
+        in_specs=[hbm if outside else vmem] * len(operands),
         out_specs=[vmem] * len(shapes),
         scratch_shapes=scratch,
-        compiler_params=pltpu.CompilerParams(vmem_limit_bytes=limit),
+        compiler_params=pltpu.CompilerParams(vmem_limit_bytes=8 << 20),
         name=body.__name__,
     )(*operands)
+
+
+def array(*shape, dtype=F32):
+    return jax.ShapeDtypeStruct(shape, dtype)
 
 
 def local(field, gamma, kappa_zonal, kappa_merid, area, sea_mask, fold_pair):
     levels, height, width = field.shape
     lanes = levels * width
     devices_x, devices_y = lax.axis_size("lon"), lax.axis_size("lat")
-    tile = (height, lanes)
     count = 2 * (width - 3).bit_length()
-    operands = (field, gamma, kappa_zonal, kappa_merid, area, sea_mask)
-    scratch = [pltpu.VMEM(x.shape, x.dtype) for x in operands] + [pltpu.SemaphoreType.DMA((len(operands),))]
-    message, payload, factors, keep = run(
+    operands = (field, gamma, kappa_zonal, kappa_merid, area, sea_mask, fold_pair)
+    scratch = [pltpu.VMEM(x.shape, x.dtype) for x in operands[:-1]]
+    scratch += [pltpu.SMEM(fold_pair.shape, fold_pair.dtype), pltpu.SemaphoreType.DMA((len(operands),))]
+    message, payload, factors, keep, turn = run(
         block_local,
-        [(devices_x * devices_y, 4, lanes), (5,) + tile, (count,) + tile, (4,) + tile],
+        [
+            array(devices_x * devices_y, 4, lanes),
+            array(5, height, lanes),
+            array(count, height, lanes),
+            array(4, height, lanes),
+            array(devices_x, lanes, dtype=jnp.int32),
+        ],
         *operands,
-        outside=range(len(operands)),
+        outside=True,
         scratch=scratch,
-        limit=None,
     )
     ring_rows = lax.all_to_all(message, ("lon", "lat"), split_axis=0, concat_axis=0, tiled=True)
     ring_rows = ring_rows.reshape(devices_x, devices_y, 4, lanes)
     payload = lax.all_gather(payload, "lat", axis=0, tiled=False)
     kept, message = run(
-        column_join, [(2,) + tile, (devices_x, 2 * height + 8, lanes)], ring_rows, payload, keep
+        column_join,
+        [array(2, height, lanes), array(devices_x, 2 * height + 8, lanes)],
+        ring_rows, payload, keep,
     )
     gathered = lax.all_to_all(message, "lon", split_axis=0, concat_axis=0, tiled=True)
     (result,) = run(
-        zonal_close, [(levels, height, width)], gathered, ring_rows, kept, factors, keep, fold_pair, scalars=(5,)
+        zonal_close, [array(levels, height, width)], gathered, ring_rows, kept, factors, keep, turn
     )
     return result
 

time: 37.5 us -> 35.3 us (0.941)
  Pallas kernels: 6.23 us -> 5.09 us
  local copies, waits for them, and re-layouts: 0.66 us -> 0 us
  blocking collectives: 22.4 us -> 22 us
    pallas_call x3, Pallas kernels: 6.23 us -> 5.09 us  [run(): pl.pallas_call(body, out_shape=shapes, in_specs=[hbm if outside else vmem...]
    unnamed x8 -> x0, local copies, waits for them, and re-layouts: 0.66 us -> none
where the time goes in v3:
time: 35.3 us; the launch traced here: 35.1 us
  blocking collectives  22 us (62%)
  starting transfers between devices  7.3 us (21%)
  Pallas kernels  5.09 us (14%)
  waiting for transfers between devices  0.61 us (2%)
    all_to_all x1, blocking collectives, local(): lax.all_to_all(message, 'lon', split_axis=0, concat_axis=0, tiled=True)  15.2 us
    all_to_all x1, starting transfers between devices, local(): lax.all_to_all(message, ('lon', 'lat'), split_axis=0, concat_axis=0, tile...  7.3 us
    all_gather x1, blocking collectives, local(): payload = lax.all_gather(payload, 'lat', axis=0, tiled=False)  6.8 us
    pallas_call x3, Pallas kernels, run(): pl.pallas_call(body, out_shape=shapes, in_specs=[hbm if outside else vmem...  5.09 us
  transfers between devices with their start and end apart: 1, of which 1 were waited for; matrix products, arithmetic and copies ran while one was open for 0% of the time, Pallas kernels for 0%

profile of v3, /device:TPU:0, one launch (start us, length us, event | category | flops | bytes accessed | tf_op | source)
XLA Modules:
  0.0 35.1 jit_solution(1270931485275802663)
XLA Ops:
  0.0 2.7 %block_local.1 = (f32[32,4,128]{2,1,0:T(4,128)}, f32[5,32,128]{2,1,0:T(8,128)S(1)}, f32[12,32,128]{2,1,0:T(8,128)S(1)}, f32[4,32,128]{2,1,0:T(8,128)S(1)}, s32[8,128]{1,0:T(8,128)S(1)}) custom-call(f32[2,32,64]{2,1,0:T(8,128)} %refs_0_.1, f32[2,32,64]{2,1,0:T(8,128)} %refs_1_.1, f32[2,32,64]{2,1,0:T(8,128)} %refs_2_.1, f32[2,32,64]{2,1,0:T(8,128)} %refs_3_.1, ...), custom_call_target="tpu_custom_call" | custom-call | tf_op jit(solution)/shard_map/block_local/pallas_call | solution.py:321
  2.7 7.3 %all-to-all-start = ((f32[32,4,128]{2,1,0:T(4,128)}), f32[32,4,128]{2,1,0:T(4,128)S(1)}, u32[]{:S(2)}, u32[]{:S(2)}) async-start(f32[32,4,128]{2,1,0:T(4,128)} %get-tuple-element.12), calls=%async_computation | async-start | bytes 131072 | tf_op jit(solution)/shard_map/all_to_all | solution.py:357
  10.0 6.8 %all-gather = f32[20,32,128]{2,1,0:T(8,128)S(1)} all-gather(f32[5,32,128]{2,1,0:T(8,128)S(1)} %get-tuple-element.13), channel_id=2, replica_groups=mesh['lon'=8,'lat'=4] {'lat'}, dimensions={0}, use_global_device_ids=true | all-gather | bytes 409600 | tf_op jit(solution)/shard_map/all_gather | solution.py:359
  16.8 0.6 %all-to-all-done = f32[32,4,128]{2,1,0:T(4,128)S(1)} async-done(((f32[32,4,128]{2,1,0:T(4,128)}), f32[32,4,128]{2,1,0:T(4,128)S(1)}, u32[]{:S(2)}, u32[]{:S(2)}) %all-to-all-start) | async-done | bytes 65568 | tf_op jit(solution)/shard_map/all_to_all | solution.py:357
  17.4 0.9 %column_join.1 = (f32[2,32,128]{2,1,0:T(8,128)S(1)}, f32[8,72,128]{2,1,0:T(8,128)S(1)}) custom-call(f32[8,4,4,128]{3,2,1,0:T(4,128)S(1)} %bitcast.3, f32[4,5,32,128]{3,2,1,0:T(8,128)S(1)} %bitcast.2, f32[4,32,128]{2,1,0:T(8,128)S(1)} %get-tuple-element.14.keep), custom_call_target="tpu_custom_call" | custom-call | tf_op jit(solution)/shard_map/column_join/pallas_call | solution.py:321
  18.4 15.2 %all_to_all.10.gathered = f32[8,72,128]{2,1,0:T(8,128)S(1)} all-to-all(f32[8,72,128]{2,1,0:T(8,128)S(1)} %get-tuple-element.15), channel_id=1, replica_groups=mesh['lon'=8,'lat'=4] {'lon'}, dimensions={0} | all-to-all | bytes 589824 | tf_op jit(solution)/shard_map/all_to_all | solution.py:365
  33.6 1.4 %zonal_close.1 = f32[2,32,64]{2,1,0:T(8,128)} custom-call(f32[8,72,128]{2,1,0:T(8,128)S(1)} %all_to_all.10.gathered, f32[8,4,4,128]{3,2,1,0:T(4,128)S(1)} %bitcast.4, f32[2,32,128]{2,1,0:T(8,128)S(1)} %get-tuple-element.16.kept, f32[12,32,128]{2,1,0:T(8,128)S(1)} %get-tuple-element.17.factors_ref, f32[4,32,128]{2,1,0:T(8,128)S(1)} %get-tuple-element.14.keep, ...), custom_call_target="tpu_custom_call" | custom-call | tf_op jit(solution)/shard_map/zonal_close/pallas_call | solution.py:321
Async XLA Ops:
  2.7 14.7 %all-to-all-start = ((f32[32,4,128]{2,1,0:T(4,128)}), f32[32,4,128]{2,1,0:T(4,128)S(1)}, u32[]{:S(2)}, u32[]{:S(2)}) async-start(f32[32,4,128]{2,1,0:T(4,128)} %get-tuple-element.12), calls=%async_computation | async-start | bytes 131072 | tf_op jit(solution)/shard_map/all_to_all | solution.py:357

commit v4 on v3

--- a/solution.py
+++ b/solution.py
@@ -95,17 +95,9 @@
         copy.wait()
 
 
-def block_local(*refs):
-    sources, (message, payload, factors_out, keep, turn), buffers, semaphores = (
-        refs[:7], refs[7:12], refs[12:19], refs[19]
-    )
-    fetch(sources, buffers, semaphores)
-    field, gamma, kappa_zonal, kappa_merid, area, mask, pairing = buffers
+def zonal_block(field, gamma, kappa_zonal, ocean):
     levels, height, width = field.shape
-    lanes = levels * width
-    ocean_one = mask[...].astype(F32)
-    ocean = jnp.concatenate([ocean_one] * levels, axis=1)
-    place = iota((height, lanes), 1) % width
+    place = iota((height, levels * width), 1) % width
     scaled = beside(gamma) * ocean
     source = scaled * beside(field)
     open_face = beside(kappa_zonal) * ocean
@@ -125,20 +117,33 @@
     edge = to_first * last
     first = jnp.where(place == 0, 1.0, first)
     last = jnp.where(place == width - 1, 1.0, last)
-    rows = half_sums(
-        [
-            first * source,
-            last * source,
-            first,
-            last,
-            edge,
-            jnp.where(place == width - 1, open_face, 0.0),
-            jnp.where(place == 0, ocean, 0.0),
-        ],
-        levels,
-    )
+    outward = jnp.where(place == width - 1, open_face, 0.0)
+    terms = [first * source, first, edge, last * source, last, outward]
+    return factors, scaled, inverse, direct * inverse, first, last, terms
+
+
+def unpack(refs):
+    sources, outputs, buffers, semaphores = refs[:7], refs[7:12], refs[12:19], refs[19]
+    fetch(sources, buffers, semaphores)
+    return outputs, buffers
+
+
+def fold_sum(pairing, width):
+    return pairing[0] + lax.axis_index("lon") * width
+
+
+def block_local(*refs):
+    (message, payload, factors_out, keep, turn), buffers = unpack(refs)
+    field, gamma, kappa_zonal, kappa_merid, area, mask, pairing = buffers
+    levels, height, width = field.shape
+    ocean_one = mask[...].astype(F32)
+    ocean = jnp.concatenate([ocean_one] * levels, axis=1)
+    factors, scaled, inverse, direct, first, last, terms = zonal_block(field, gamma, kappa_zonal, ocean)
+    place = iota(first.shape, 1) % width
+    order = [terms[0], terms[3], terms[1], terms[4], terms[2], terms[5]]
+    rows = half_sums(order + [jnp.where(place == 0, ocean, 0.0)], levels)
     message[...] = jnp.broadcast_to(jnp.concatenate([rows[:4], rows[4:]], axis=1)[None], message.shape)
-    payload[0] = direct * inverse
+    payload[0] = direct
     payload[1] = first
     payload[2] = last
     payload[3] = beside(kappa_merid) * ocean
@@ -148,7 +153,7 @@
     keep[1] = last
     keep[2] = inverse
     keep[3] = scaled
-    turn[...] = jnp.full(turn.shape, pairing[0] + lax.axis_index("lon") * width, jnp.int32)
+    turn[...] = jnp.full(turn.shape, fold_sum(pairing, width), jnp.int32)
 
 
 def ring_setup(first_ground, last_ground, edge, open_face, ocean):
@@ -304,11 +309,11 @@
     inner = keep[2] > 0.0
     direct = relax(jnp.where(inner, current, 0.0), load_factors(factors_ref), 1) * keep[2]
 
-    def ends(values):
-        own = own_row(values, index_x)
-        return columns(jnp.concatenate([own, own], axis=1)[:, :lanes], 0, height, levels, lanes)
-
-    result = keep[3] * (direct + keep[0] * ends(first_ends) + keep[1] * ends(last_ends))
+    result = keep[3] * (
+        direct
+        + keep[0] * spread_ends(first_ends, index_x, height, levels, lanes)
+        + keep[1] * spread_ends(last_ends, index_x, height, levels, lanes)
+    )
     for k in range(levels):
         out[k] = result[:, k * width : (k + 1) * width]
 
@@ -333,6 +338,237 @@
     return jax.ShapeDtypeStruct(shape, dtype)
 
 
+def column_order(place, width):
+    return jnp.where(place < width // 2, place, width + width // 2 - 1 - place)
+
+
+def block_send(*refs):
+    (message, factors_out, keep, turn), buffers = unpack_four(refs)
+    field, gamma, kappa_zonal, kappa_merid, area, mask, pairing = buffers
+    levels, height, width = field.shape
+    lanes = levels * width
+    half = width // 2
+    ocean_one = mask[...].astype(F32)
+    ocean = jnp.concatenate([ocean_one] * levels, axis=1)
+    factors, scaled, inverse, direct, first, last, terms = zonal_block(field, gamma, kappa_zonal, ocean)
+    devices = message.shape[0]
+    centre = (fold_sum(pairing, width) % (lax.axis_size("lon") * width) + 1) // 2
+    row = iota((height, lanes), 0)
+    merid = beside(kappa_merid) * jnp.where(row == height - 1, ocean, ocean * moved(ocean, -1, 0))
+    lane = iota((height, lanes), 1)
+    reach = lane // width * width + (column_order(lane % width, width) + centre) % width
+
+    def ordered(values):
+        return jnp.take_along_axis(values, reach, axis=1)
+
+    pieces = jnp.concatenate([ordered(x) for x in (direct, first, last, merid)], axis=0).T
+    for k, start in enumerate((0, width, half, width + half)):
+        message[:, k, :] = pieces[start : start + devices]
+    packed = ordered(jnp.concatenate([1.0 / area[...], ocean_one], axis=1))
+
+    def tile(distance):
+        return jnp.broadcast_to(moved(packed, distance, 1)[:1], (8, lanes))
+
+    extra = jnp.concatenate(
+        [
+            packed,
+            jnp.broadcast_to(ocean_one[:, :1], (height, lanes)),
+            tile(-width - half),
+            moved(packed, -half, 1),
+            jnp.zeros((lanes - 3 * height - 16, lanes), F32),
+            tile(-width),
+        ],
+        axis=0,
+    ).T
+    message[:, 4, :] = extra[:devices]
+    rows = half_sums(terms, levels)
+    for k in range(3):
+        both = jnp.concatenate([rows[k : k + 1], rows[k + 3 : k + 4]], axis=1)
+        message[:, 5 + k, :] = jnp.broadcast_to(both, (devices, lanes))
+    store_factors(factors_out, factors)
+    keep[0] = first
+    keep[1] = last
+    keep[2] = inverse
+    keep[3] = scaled
+    turn[...] = jnp.full(turn.shape, centre, jnp.int32)
+
+
+def unpack_four(refs):
+    sources, outputs, buffers, semaphores = refs[:7], refs[7:11], refs[11:18], refs[18]
+    fetch(sources, buffers, semaphores)
+    return outputs, buffers
+
+
+def column_solve(gathered, turn, message, hold):
+    devices_x, devices_y, tall, lanes = gathered.shape
+    height = lanes // devices_y
+    width = devices_x * devices_y * 2
+    levels = 2
+    shape = (devices_x * tall, lanes)
+    small = iota((devices_x, lanes), 1) // height
+    lane = iota(shape, 1)
+    line = iota(shape, 0) % tall
+    lats = range(devices_y)
+
+    def merged(parts, where, target):
+        result = None
+        for k, values in enumerate(parts):
+            turned = moved(values, (k - where[k]) * height, 1)
+            result = turned if k == 0 else jnp.where(target == k, turned, result)
+        return result
+
+    def ring_term(r, f):
+        parts = [gathered[:, y, r, :] for y in lats]
+        return jnp.concatenate(
+            [merged(parts, [f * levels + h] * devices_y, small) for h in range(levels)], axis=1
+        )
+
+    first_source, last_source = ring_term(5, 0), ring_term(5, 1)
+    first_ground, last_ground = ring_term(6, 0), ring_term(6, 1)
+    edge, open_face = ring_term(7, 0), ring_term(7, 1)
+    ocean = merged([gathered[:, y, 4, :] for y in lats], [1] * devices_y, small)
+    ring = ring_setup(first_ground, last_ground, edge, open_face, jnp.concatenate([ocean] * levels, axis=1))
+    first_ends, last_ends = ring_ends(first_source, last_source, *ring)
+
+    def at_columns(ends):
+        even = iota((tall, lanes), 0) % levels == 0
+        return jnp.concatenate(
+            [jnp.where(even, ends[b : b + 1, :lanes], ends[b : b + 1, lanes:]) for b in range(devices_x)], axis=0
+        )
+
+    tiles = [gathered[:, y, :, :].reshape(shape) for y in lats]
+    direct, first, last, faces = [merged(tiles, [k] * devices_y, lane // height) for k in range(4)]
+    used = line < 4
+    current = jnp.where(used, direct + first * at_columns(first_ends) + last * at_columns(last_ends), 0.0)
+    reciprocal, beyond = jnp.ones(shape, F32), jnp.zeros(shape, F32)
+    for y in lats:
+        extra = jnp.broadcast_to(gathered[:, y, 4:5, :], (devices_x, tall, lanes)).reshape(shape)
+        turned = jnp.where(
+            line < 2, moved(extra, y * height, 1), moved(extra, (y - 2) * height - 8, 1)
+        )
+        reciprocal = jnp.where(lane // height == y, turned, reciprocal)
+        if y > 0:
+            beyond = jnp.where(lane == y * height - 1, turned, beyond)
+    faces = jnp.where(used, jnp.where(lane % height == height - 1, faces * beyond, faces), 0.0)
+    factors, (ground, current) = condense(
+        moved(faces, 1, 1), faces, [jnp.ones(shape, F32), current], lanes, 1
+    )
+    inverse = 1.0 / ground
+    current = current * inverse
+
+    index = lax.axis_index("lon") * devices_y + lax.axis_index("lat")
+    centre = turn[...]
+    block, place = centre // width, centre % width
+    offset = devices_x - 1 + 2 * block
+    offset = offset + (index + place >= width).astype(jnp.int32) + (place - 1 - index >= 0).astype(jnp.int32)
+
+    def across(values):
+        parts = []
+        for b in range(devices_x):
+            wanted = (offset - b + devices_x) % devices_x
+            part = values[:tall]
+            for k in range(1, devices_x):
+                part = jnp.where(wanted == k, values[k * tall : (k + 1) * tall], part)
+            parts.append(part)
+        other = jnp.concatenate(parts, axis=0)
+        return jnp.where(line < 2, moved(other, -2, 0), moved(other, 2, 0))
+
+    folded = 0.25 * (current + across(current)) * (reciprocal + across(reciprocal))
+    current = jnp.where(lane == lanes - 1, folded, current * reciprocal)
+    current = relax(current, factors, 1) * inverse
+
+    first, last = first * current, last * current
+    first, last = first + moved(first, -2, 0), last + moved(last, -2, 0)
+    hold[0] = jnp.where(line < 2, first, moved(last, 2, 0)).reshape(hold.shape[1:])
+    hold[1] = current.reshape(hold.shape[1:])
+    row = iota((devices_x, lanes), 0)
+    for y in lats:
+        ends, own = [
+            merged([hold[k, :, r, :] for r in range(4)], [y] * 4, small) for k in range(2)
+        ]
+        for b in range(devices_x):
+            message[b, y] = jnp.where(row == b, own, ends)
+
+
+def block_close(gathered, ring_rows, factors_ref, keep, turn, out):
+    levels, height, width = out.shape
+    lanes = levels * width
+    lines = levels * height
+    half = width // 2
+    devices = gathered.shape[0]
+    index_x, index_y = lax.axis_index("lon"), lax.axis_index("lat")
+    mine = ring_rows[:, pl.ds(index_y, 1), :, :].reshape(ring_rows.shape[0], ring_rows.shape[2], lanes)
+    ocean = mine[:, 4, height : 2 * height]
+    ring = ring_setup(
+        mine[:, 6, :lines],
+        mine[:, 6, lines:],
+        mine[:, 7, :lines],
+        mine[:, 7, lines:],
+        jnp.concatenate([ocean] * levels, axis=1),
+    )
+    own = gathered[:, pl.ds(index_x, 1), :].reshape(devices, lanes)
+    turned = jnp.concatenate([moved(own, -k * height, 1) for k in (0, 2, 1, 3)], axis=0).T[:height]
+    lane = iota((height, lanes), 1)
+    centre = jnp.broadcast_to(turn[:1], (height, lanes))
+    reach = lane // width * width + column_order((lane - centre + 8 * width) % width, width)
+    current = jnp.take_along_axis(turned, reach, axis=1)
+    sums = jnp.sum(gathered[...], axis=0)
+    rows = half_sums([keep[0] * current, keep[1] * current], levels)
+    chosen = iota((sums.shape[0], lines), 0) == index_x
+    first_source = jnp.where(chosen, rows[:1], sums[:, :lines])
+    last_source = jnp.where(chosen, rows[1:2], sums[:, lines:])
+    first_ends, last_ends = ring_ends(first_source, last_source, *ring)
+    inner = keep[2] > 0.0
+    direct = relax(jnp.where(inner, current, 0.0), load_factors(factors_ref), 1) * keep[2]
+    result = keep[3] * (
+        direct
+        + keep[0] * spread_ends(first_ends, index_x, height, levels, lanes)
+        + keep[1] * spread_ends(last_ends, index_x, height, levels, lanes)
+    )
+    for k in range(levels):
+        out[k] = result[:, k * width : (k + 1) * width]
+
+
+def spread_ends(values, index, height, levels, lanes):
+    own = own_row(values, index)
+    return columns(jnp.concatenate([own, own], axis=1)[:, :lanes], 0, height, levels, lanes)
+
+
+def local_by_columns(operands, scratch, count):
+    levels, height, width = operands[0].shape
+    lanes = levels * width
+    devices_x, devices_y = lax.axis_size("lon"), lax.axis_size("lat")
+    devices = devices_x * devices_y
+    message, factors, keep, turn = run(
+        block_send,
+        [
+            array(devices, 8, lanes),
+            array(count, height, lanes),
+            array(4, height, lanes),
+            array(8, lanes, dtype=jnp.int32),
+        ],
+        *operands,
+        outside=True,
+        scratch=scratch,
+    )
+    both = ("lon", "lat")
+    ring_rows = lax.all_to_all(message, both, split_axis=0, concat_axis=0, tiled=True)
+    ring_rows = ring_rows.reshape(devices_x, devices_y, 8, lanes)
+    (message,) = run(
+        column_solve,
+        [array(devices_x, devices_y, devices_x, lanes)],
+        ring_rows,
+        turn,
+        scratch=[pltpu.VMEM((2, devices_x, 8, lanes), F32)],
+    )
+    message = message.reshape(devices, devices_x, lanes)
+    gathered = lax.all_to_all(message, both, split_axis=0, concat_axis=0, tiled=True)
+    (result,) = run(
+        block_close, [array(levels, height, width)], gathered, ring_rows, factors, keep, turn
+    )
+    return result
+
+
 def local(field, gamma, kappa_zonal, kappa_merid, area, sea_mask, fold_pair):
     levels, height, width = field.shape
     lanes = levels * width
@@ -341,6 +577,8 @@
     operands = (field, gamma, kappa_zonal, kappa_merid, area, sea_mask, fold_pair)
     scratch = [pltpu.VMEM(x.shape, x.dtype) for x in operands[:-1]]
     scratch += [pltpu.SMEM(fold_pair.shape, fold_pair.dtype), pltpu.SemaphoreType.DMA((len(operands),))]
+    if width == 2 * devices_x * devices_y and levels == 2 and devices_y * height == lanes == 4 * height:
+        return local_by_columns(operands, scratch, count)
     message, payload, factors, keep, turn = run(
         block_local,
         [

time: 35.3 us -> 30.7 us (0.87)
  starting transfers between devices: 7.3 us -> 0 us
  blocking collectives: 22 us -> 25.3 us
  waiting for transfers between devices: 0.61 us -> 0 us
    all_to_all x1 -> x2, blocking collectives: 15.2 us -> 25.3 us  [local_by_columns(): lax.all_to_all(message, both, split_axis=0, concat_axis=0, tiled=True)]
    all_to_all x1 -> x0, starting transfers between devices: 7.3 us -> none  [local(): lax.all_to_all(message, ('lon', 'lat'), split_axis=0, concat_axis=0, tile...]
    all_gather x1 -> x0, blocking collectives: 6.8 us -> none  [local(): payload = lax.all_gather(payload, 'lat', axis=0, tiled=False)]
    all_to_all x1 -> x0, waiting for transfers between devices: 0.61 us -> none  [local(): lax.all_to_all(message, ('lon', 'lat'), split_axis=0, concat_axis=0, tile...]
  transfers between devices with their start and end apart: 1 -> 0, of which waited for: 1 -> 0; matrix products, arithmetic and copies ran while one was open for 0% -> 0% of each run, Pallas kernels for 0% -> 0%
where the time goes in v4:
time: 30.7 us; the launch traced here: 30.5 us
  blocking collectives  25.3 us (82%)
  Pallas kernels  5.12 us (17%)
    all_to_all x2, blocking collectives, local_by_columns(): lax.all_to_all(message, both, split_axis=0, concat_axis=0, tiled=True)  25.3 us
    pallas_call x3, Pallas kernels, run(): pl.pallas_call(body, out_shape=shapes, in_specs=[hbm if outside else vmem...  5.12 us

profile of v4, /device:TPU:0, one launch (start us, length us, event | category | flops | bytes accessed | tf_op | source)
XLA Modules:
  0.0 30.5 jit_solution(7434236846513819244)
XLA Ops:
  0.0 2.2 %block_send.1 = (f32[32,8,128]{2,1,0:T(8,128)S(1)}, f32[12,32,128]{2,1,0:T(8,128)S(1)}, f32[4,32,128]{2,1,0:T(8,128)S(1)}, s32[8,128]{1,0:T(8,128)S(1)}) custom-call(f32[2,32,64]{2,1,0:T(8,128)} %refs_0_.1, f32[2,32,64]{2,1,0:T(8,128)} %refs_1_.1, f32[2,32,64]{2,1,0:T(8,128)} %refs_2_.1, f32[2,32,64]{2,1,0:T(8,128)} %refs_3_.1, f32[32,64]{1,0:T(8,128)} %refs_4_.1, ...), custom_call_target="tpu_custom_call" | custom-call | tf_op jit(solution)/shard_map/block_send/pallas_call | solution.py:326
  2.2 15.3 %all_to_all.10 = f32[32,8,128]{2,1,0:T(8,128)S(1)} all-to-all(f32[32,8,128]{2,1,0:T(8,128)S(1)} %get-tuple-element.9), channel_id=1, replica_groups=mesh['lon'=8,'lat'=4] {'lon','lat'}, dimensions={0} | all-to-all | bytes 262144 | tf_op jit(solution)/shard_map/all_to_all | solution.py:555
  17.5 1.6 %column_solve.1 = f32[8,4,8,128]{3,2,1,0:T(8,128)S(1)} custom-call(f32[8,4,8,128]{3,2,1,0:T(8,128)S(1)} %bitcast.2, s32[8,128]{1,0:T(8,128)S(1)} %get-tuple-element.10.turn), custom_call_target="tpu_custom_call" | custom-call | tf_op jit(solution)/shard_map/column_solve/pallas_call | solution.py:326
  19.1 10.0 %all_to_all.11.gathered = f32[32,8,128]{2,1,0:T(8,128)S(1)} all-to-all(f32[32,8,128]{2,1,0:T(8,128)S(1)} %bitcast.4), channel_id=1, replica_groups=mesh['lon'=8,'lat'=4] {'lon','lat'}, dimensions={0} | all-to-all | bytes 262144 | tf_op jit(solution)/shard_map/all_to_all | solution.py:565
  29.1 1.3 %block_close.1 = f32[2,32,64]{2,1,0:T(8,128)} custom-call(f32[32,8,128]{2,1,0:T(8,128)S(1)} %all_to_all.11.gathered, f32[8,4,8,128]{3,2,1,0:T(8,128)S(1)} %bitcast.3, f32[12,32,128]{2,1,0:T(8,128)S(1)} %get-tuple-element.11.factors_ref, f32[4,32,128]{2,1,0:T(8,128)S(1)} %get-tuple-element.12.keep, s32[8,128]{1,0:T(8,128)S(1)} %get-tuple-element.10.turn), custom_call_target="tpu_custom_call" | custom-call | tf_op jit(solution)/shard_map/block_close/pallas_call | solution.py:326

commit v5 on v4

--- a/solution.py
+++ b/solution.py
@@ -13,7 +13,8 @@
 
 
 def moved(values, distance, axis):
-    return pltpu.roll(values, distance % values.shape[axis], axis)
+    distance %= values.shape[axis]
+    return pltpu.roll(values, distance, axis) if distance else values
 
 
 def iota(shape, axis):
@@ -122,8 +123,8 @@
     return factors, scaled, inverse, direct * inverse, first, last, terms
 
 
-def unpack(refs):
-    sources, outputs, buffers, semaphores = refs[:7], refs[7:12], refs[12:19], refs[19]
+def unpack(refs, count):
+    sources, outputs, buffers, semaphores = refs[:7], refs[7 : 7 + count], refs[7 + count : 14 + count], refs[14 + count]
     fetch(sources, buffers, semaphores)
     return outputs, buffers
 
@@ -133,7 +134,7 @@
 
 
 def block_local(*refs):
-    (message, payload, factors_out, keep, turn), buffers = unpack(refs)
+    (message, payload, factors_out, keep, turn), buffers = unpack(refs, 5)
     field, gamma, kappa_zonal, kappa_merid, area, mask, pairing = buffers
     levels, height, width = field.shape
     ocean_one = mask[...].astype(F32)
@@ -343,7 +344,7 @@
 
 
 def block_send(*refs):
-    (message, factors_out, keep, turn), buffers = unpack_four(refs)
+    (message, factors_out, keep, turn), buffers = unpack(refs, 4)
     field, gamma, kappa_zonal, kappa_merid, area, mask, pairing = buffers
     levels, height, width = field.shape
     lanes = levels * width
@@ -381,10 +382,13 @@
         axis=0,
     ).T
     message[:, 4, :] = extra[:devices]
-    rows = half_sums(terms, levels)
-    for k in range(3):
-        both = jnp.concatenate([rows[k : k + 1], rows[k + 3 : k + 4]], axis=1)
-        message[:, 5 + k, :] = jnp.broadcast_to(both, (devices, lanes))
+    wide = jnp.concatenate([terms[0], terms[3], terms[2], terms[5]], axis=0).T
+    sums = level_sums(wide, levels)
+    grounds = level_sums(pieces, levels)
+    middle = iota((1, lanes), 1) // height
+    grounds = jnp.where((middle == 1) | (middle == 2), grounds[0], moved(grounds[1], 2 * height, 1))
+    for k, values in enumerate((*sums, grounds)):
+        message[:, 5 + k, :] = jnp.broadcast_to(values, (devices, lanes))
     store_factors(factors_out, factors)
     keep[0] = first
     keep[1] = last
@@ -393,10 +397,13 @@
     turn[...] = jnp.full(turn.shape, centre, jnp.int32)
 
 
-def unpack_four(refs):
-    sources, outputs, buffers, semaphores = refs[:7], refs[7:11], refs[11:18], refs[18]
-    fetch(sources, buffers, semaphores)
-    return outputs, buffers
+def level_sums(values, levels):
+    part = values.shape[0] // levels
+    return [jnp.sum(values[k * part : (k + 1) * part], axis=0, keepdims=True) for k in range(levels)]
+
+
+def ring_place(k, level):
+    return (5 + level, k) if k < 4 else (7, (1 + k - 4 + 2 * level) % 4)
 
 
 def column_solve(gathered, turn, message, hold):
@@ -404,10 +411,13 @@
     height = lanes // devices_y
     width = devices_x * devices_y * 2
     levels = 2
-    shape = (devices_x * tall, lanes)
+    pairs = devices_x // 2
+    shape = (pairs * tall, lanes)
     small = iota((devices_x, lanes), 1) // height
     lane = iota(shape, 1)
     line = iota(shape, 0) % tall
+    lower = line < 4
+    outer = line % 4 < 2
     lats = range(devices_y)
 
     def merged(parts, where, target):
@@ -417,39 +427,47 @@
             result = turned if k == 0 else jnp.where(target == k, turned, result)
         return result
 
-    def ring_term(r, f):
-        parts = [gathered[:, y, r, :] for y in lats]
-        return jnp.concatenate(
-            [merged(parts, [f * levels + h] * devices_y, small) for h in range(levels)], axis=1
-        )
-
-    first_source, last_source = ring_term(5, 0), ring_term(5, 1)
-    first_ground, last_ground = ring_term(6, 0), ring_term(6, 1)
-    edge, open_face = ring_term(7, 0), ring_term(7, 1)
+    def ring_term(k):
+        parts = []
+        for level in range(levels):
+            r, group = ring_place(k, level)
+            parts.append(merged([gathered[:, y, r, :] for y in lats], [group] * devices_y, small))
+        return jnp.concatenate(parts, axis=1)
+
+    first_source, last_source, edge, open_face, first_ground, last_ground = [ring_term(k) for k in range(6)]
     ocean = merged([gathered[:, y, 4, :] for y in lats], [1] * devices_y, small)
     ring = ring_setup(first_ground, last_ground, edge, open_face, jnp.concatenate([ocean] * levels, axis=1))
     first_ends, last_ends = ring_ends(first_source, last_source, *ring)
 
     def at_columns(ends):
-        even = iota((tall, lanes), 0) % levels == 0
-        return jnp.concatenate(
-            [jnp.where(even, ends[b : b + 1, :lanes], ends[b : b + 1, lanes:]) for b in range(devices_x)], axis=0
-        )
-
-    tiles = [gathered[:, y, :, :].reshape(shape) for y in lats]
+        row = iota((tall, lanes), 0)
+        tiles = []
+        for b in range(pairs):
+            near, far = ends[b : b + 1], ends[b + pairs : b + pairs + 1]
+            even = jnp.where(row < 4, near[:, :lanes], far[:, :lanes])
+            odd = jnp.where(row < 4, near[:, lanes:], far[:, lanes:])
+            tiles.append(jnp.where(row % levels == 0, even, odd))
+        return jnp.concatenate(tiles, axis=0)
+
+    def paired(values):
+        near, far = values[:pairs].reshape(shape), values[pairs:].reshape(shape)
+        return jnp.where(lower, near, moved(far, 4, 0))
+
+    tiles = [paired(gathered[:, y, :, :]) for y in lats]
     direct, first, last, faces = [merged(tiles, [k] * devices_y, lane // height) for k in range(4)]
-    used = line < 4
-    current = jnp.where(used, direct + first * at_columns(first_ends) + last * at_columns(last_ends), 0.0)
-    reciprocal, beyond = jnp.ones(shape, F32), jnp.zeros(shape, F32)
+    current = direct + first * at_columns(first_ends) + last * at_columns(last_ends)
+    reciprocal, beyond = None, jnp.zeros(shape, F32)
     for y in lats:
-        extra = jnp.broadcast_to(gathered[:, y, 4:5, :], (devices_x, tall, lanes)).reshape(shape)
-        turned = jnp.where(
-            line < 2, moved(extra, y * height, 1), moved(extra, (y - 2) * height - 8, 1)
-        )
-        reciprocal = jnp.where(lane // height == y, turned, reciprocal)
+        near, far = [
+            jnp.broadcast_to(gathered[k : k + pairs, y, 4:5, :], (pairs, tall, lanes)).reshape(shape)
+            for k in (0, pairs)
+        ]
+        extra = jnp.where(lower, near, far)
+        turned = jnp.where(outer, moved(extra, y * height, 1), moved(extra, (y - 2) * height - 8, 1))
+        reciprocal = turned if y == 0 else jnp.where(lane // height == y, turned, reciprocal)
         if y > 0:
             beyond = jnp.where(lane == y * height - 1, turned, beyond)
-    faces = jnp.where(used, jnp.where(lane % height == height - 1, faces * beyond, faces), 0.0)
+    faces = jnp.where(lane % height == height - 1, faces * beyond, faces)
     factors, (ground, current) = condense(
         moved(faces, 1, 1), faces, [jnp.ones(shape, F32), current], lanes, 1
     )
@@ -464,14 +482,14 @@
 
     def across(values):
         parts = []
-        for b in range(devices_x):
+        for b in range(pairs):
             wanted = (offset - b + devices_x) % devices_x
             part = values[:tall]
-            for k in range(1, devices_x):
-                part = jnp.where(wanted == k, values[k * tall : (k + 1) * tall], part)
-            parts.append(part)
+            for k in range(1, pairs):
+                part = jnp.where(wanted % pairs == k, values[k * tall : (k + 1) * tall], part)
+            parts.append(jnp.where(wanted >= pairs, moved(part, 4, 0), part))
         other = jnp.concatenate(parts, axis=0)
-        return jnp.where(line < 2, moved(other, -2, 0), moved(other, 2, 0))
+        return jnp.where(outer, moved(other, -2, 0), moved(other, 2, 0))
 
     folded = 0.25 * (current + across(current)) * (reciprocal + across(reciprocal))
     current = jnp.where(lane == lanes - 1, folded, current * reciprocal)
@@ -479,52 +497,33 @@
 
     first, last = first * current, last * current
     first, last = first + moved(first, -2, 0), last + moved(last, -2, 0)
-    hold[0] = jnp.where(line < 2, first, moved(last, 2, 0)).reshape(hold.shape[1:])
-    hold[1] = current.reshape(hold.shape[1:])
-    row = iota((devices_x, lanes), 0)
+    for k, values in enumerate((jnp.where(outer, first, moved(last, 2, 0)), current)):
+        for b in range(pairs):
+            tile = values[b * tall : (b + 1) * tall]
+            hold[k, b] = tile
+            hold[k, b + pairs] = moved(tile, 4, 0)
+    sources = [jnp.concatenate([hold[0, :, k, :], hold[0, :, k + 1, :]], axis=1) for k in (0, 2)]
+    ends = ring_ends(*sources, *ring)
+    ends = [part[:, k * lanes : (k + 1) * lanes] for part in ends for k in range(levels)]
+    own = [hold[1, :, k, :] for k in range(4)]
     for y in lats:
-        ends, own = [
-            merged([hold[k, :, r, :] for r in range(4)], [y] * 4, small) for k in range(2)
-        ]
-        for b in range(devices_x):
-            message[b, y] = jnp.where(row == b, own, ends)
-
-
-def block_close(gathered, ring_rows, factors_ref, keep, turn, out):
+        message[:, y, 0, :] = merged(own, [y] * 4, small)
+        message[:, y, 1, :] = merged(ends, [y] * 4, small)
+
+
+def block_close(gathered, factors_ref, keep, turn, out):
     levels, height, width = out.shape
     lanes = levels * width
-    lines = levels * height
-    half = width // 2
-    devices = gathered.shape[0]
-    index_x, index_y = lax.axis_index("lon"), lax.axis_index("lat")
-    mine = ring_rows[:, pl.ds(index_y, 1), :, :].reshape(ring_rows.shape[0], ring_rows.shape[2], lanes)
-    ocean = mine[:, 4, height : 2 * height]
-    ring = ring_setup(
-        mine[:, 6, :lines],
-        mine[:, 6, lines:],
-        mine[:, 7, :lines],
-        mine[:, 7, lines:],
-        jnp.concatenate([ocean] * levels, axis=1),
-    )
-    own = gathered[:, pl.ds(index_x, 1), :].reshape(devices, lanes)
+    own, ends = gathered[:, 0, :], jnp.sum(gathered[:, 1, :], axis=0, keepdims=True)
     turned = jnp.concatenate([moved(own, -k * height, 1) for k in (0, 2, 1, 3)], axis=0).T[:height]
     lane = iota((height, lanes), 1)
     centre = jnp.broadcast_to(turn[:1], (height, lanes))
     reach = lane // width * width + column_order((lane - centre + 8 * width) % width, width)
     current = jnp.take_along_axis(turned, reach, axis=1)
-    sums = jnp.sum(gathered[...], axis=0)
-    rows = half_sums([keep[0] * current, keep[1] * current], levels)
-    chosen = iota((sums.shape[0], lines), 0) == index_x
-    first_source = jnp.where(chosen, rows[:1], sums[:, :lines])
-    last_source = jnp.where(chosen, rows[1:2], sums[:, lines:])
-    first_ends, last_ends = ring_ends(first_source, last_source, *ring)
     inner = keep[2] > 0.0
     direct = relax(jnp.where(inner, current, 0.0), load_factors(factors_ref), 1) * keep[2]
-    result = keep[3] * (
-        direct
-        + keep[0] * spread_ends(first_ends, index_x, height, levels, lanes)
-        + keep[1] * spread_ends(last_ends, index_x, height, levels, lanes)
-    )
+    first, last = [columns(ends, k, height, levels, lanes) for k in range(2)]
+    result = keep[3] * (direct + keep[0] * first + keep[1] * last)
     for k in range(levels):
         out[k] = result[:, k * width : (k + 1) * width]
 
@@ -556,16 +555,14 @@
     ring_rows = ring_rows.reshape(devices_x, devices_y, 8, lanes)
     (message,) = run(
         column_solve,
-        [array(devices_x, devices_y, devices_x, lanes)],
+        [array(devices_x, devices_y, 2, lanes)],
         ring_rows,
         turn,
         scratch=[pltpu.VMEM((2, devices_x, 8, lanes), F32)],
     )
-    message = message.reshape(devices, devices_x, lanes)
+    message = message.reshape(devices, 2, lanes)
     gathered = lax.all_to_all(message, both, split_axis=0, concat_axis=0, tiled=True)
-    (result,) = run(
-        block_close, [array(levels, height, width)], gathered, ring_rows, factors, keep, turn
-    )
+    (result,) = run(block_close, [array(levels, height, width)], gathered, factors, keep, turn)
     return result
 
 

time: 30.7 us -> 29.4 us (0.958)
  blocking collectives: 25.3 us -> 24.4 us
    all_to_all x2, blocking collectives: 25.3 us -> 24.4 us  [local_by_columns(): lax.all_to_all(message, both, split_axis=0, concat_axis=0, tiled=True)]
where the time goes in v5:
time: 29.4 us; the launch traced here: 29.2 us
  blocking collectives  24.4 us (83%)
  Pallas kernels  4.82 us (16%)
    all_to_all x2, blocking collectives, local_by_columns(): lax.all_to_all(message, both, split_axis=0, concat_axis=0, tiled=True)  24.4 us
    pallas_call x3, Pallas kernels, run(): pl.pallas_call(body, out_shape=shapes, in_specs=[hbm if outside else vmem...  4.82 us

profile of v5, /device:TPU:0, one launch (start us, length us, event | category | flops | bytes accessed | tf_op | source)
XLA Modules:
  0.0 29.2 jit_solution(14012982856943204254)
XLA Ops:
  0.0 1.9 %block_send.1 = (f32[32,8,128]{2,1,0:T(8,128)S(1)}, f32[12,32,128]{2,1,0:T(8,128)S(1)}, f32[4,32,128]{2,1,0:T(8,128)S(1)}, s32[8,128]{1,0:T(8,128)S(1)}) custom-call(f32[2,32,64]{2,1,0:T(8,128)} %refs_0_.1, f32[2,32,64]{2,1,0:T(8,128)} %refs_1_.1, f32[2,32,64]{2,1,0:T(8,128)} %refs_2_.1, f32[2,32,64]{2,1,0:T(8,128)} %refs_3_.1, f32[32,64]{1,0:T(8,128)} %refs_4_.1, ...), custom_call_target="tpu_custom_call" | custom-call | tf_op jit(solution)/shard_map/block_send/pallas_call | solution.py:327
  2.0 15.3 %all_to_all.10 = f32[32,8,128]{2,1,0:T(8,128)S(1)} all-to-all(f32[32,8,128]{2,1,0:T(8,128)S(1)} %get-tuple-element.9), channel_id=1, replica_groups=mesh['lon'=8,'lat'=4] {'lon','lat'}, dimensions={0} | all-to-all | bytes 262144 | tf_op jit(solution)/shard_map/all_to_all | solution.py:554
  17.3 1.5 %column_solve.1 = f32[8,4,2,128]{3,2,1,0:T(2,128)S(1)} custom-call(f32[8,4,8,128]{3,2,1,0:T(8,128)S(1)} %bitcast.2, s32[8,128]{1,0:T(8,128)S(1)} %get-tuple-element.10.turn), custom_call_target="tpu_custom_call" | custom-call | tf_op jit(solution)/shard_map/column_solve/pallas_call | solution.py:327
  18.8 9.0 %all_to_all.11.gathered = f32[32,2,128]{2,1,0:T(2,128)S(1)} all-to-all(f32[32,2,128]{2,1,0:T(2,128)S(1)} %bitcast.3), channel_id=1, replica_groups=mesh['lon'=8,'lat'=4] {'lon','lat'}, dimensions={0} | all-to-all | bytes 65536 | tf_op jit(solution)/shard_map/all_to_all | solution.py:564
  27.8 1.4 %block_close.1 = f32[2,32,64]{2,1,0:T(8,128)} custom-call(f32[32,2,128]{2,1,0:T(2,128)S(1)} %all_to_all.11.gathered, f32[12,32,128]{2,1,0:T(8,128)S(1)} %get-tuple-element.11.factors_ref, f32[4,32,128]{2,1,0:T(8,128)S(1)} %get-tuple-element.12.keep, s32[8,128]{1,0:T(8,128)S(1)} %get-tuple-element.10.turn), custom_call_target="tpu_custom_call" | custom-call | tf_op jit(solution)/shard_map/block_close/pallas_call | solution.py:327

commit v6 on v5

--- a/solution.py
+++ b/solution.py
@@ -44,6 +44,26 @@
     for up, down in factors:
         values = spread(values, up, down, stride, axis)
         stride *= 2
+    return values
+
+
+def relax_by_pairs(values, factors, axis):
+    stride = 1
+    for k in range(0, len(factors), 2):
+        if k + 1 == len(factors):
+            return spread(values, *factors[k], stride, axis)
+        (up, down), (far_up, far_down) = factors[k : k + 2]
+        reach = {
+            3: moved(far_up, -stride, axis) * up,
+            2: far_up,
+            1: up + moved(far_up, stride, axis) * down,
+            -1: down + moved(far_down, -stride, axis) * up,
+            -2: far_down,
+            -3: moved(far_down, stride, axis) * down,
+        }
+        parts = [moved(factor * values, n * stride, axis) for n, factor in reach.items()]
+        values = (values + parts[1]) + (parts[0] + parts[2]) + ((parts[3] + parts[4]) + parts[5])
+        stride *= 4
     return values
 
 
@@ -493,7 +513,7 @@
 
     folded = 0.25 * (current + across(current)) * (reciprocal + across(reciprocal))
     current = jnp.where(lane == lanes - 1, folded, current * reciprocal)
-    current = relax(current, factors, 1) * inverse
+    current = relax_by_pairs(current, factors, 1) * inverse
 
     first, last = first * current, last * current
     first, last = first + moved(first, -2, 0), last + moved(last, -2, 0)
@@ -521,7 +541,7 @@
     reach = lane // width * width + column_order((lane - centre + 8 * width) % width, width)
     current = jnp.take_along_axis(turned, reach, axis=1)
     inner = keep[2] > 0.0
-    direct = relax(jnp.where(inner, current, 0.0), load_factors(factors_ref), 1) * keep[2]
+    direct = relax_by_pairs(jnp.where(inner, current, 0.0), load_factors(factors_ref), 1) * keep[2]
     first, last = [columns(ends, k, height, levels, lanes) for k in range(2)]
     result = keep[3] * (direct + keep[0] * first + keep[1] * last)
     for k in range(levels):

time: 29.4 us -> 29 us (0.986)
  Pallas kernels: 4.82 us -> 4.46 us
    pallas_call x3, Pallas kernels: 4.82 us -> 4.46 us  [run(): pl.pallas_call(body, out_shape=shapes, in_specs=[hbm if outside else vmem...]
where the time goes in v6:
time: 29 us; the launch traced here: 28.8 us
  blocking collectives  24.4 us (84%)
  Pallas kernels  4.46 us (15%)
    all_to_all x2, blocking collectives, local_by_columns(): lax.all_to_all(message, both, split_axis=0, concat_axis=0, tiled=True)  24.4 us
    pallas_call x3, Pallas kernels, run(): pl.pallas_call(body, out_shape=shapes, in_specs=[hbm if outside else vmem...  4.46 us

profile of v6, /device:TPU:0, one launch (start us, length us, event | category | flops | bytes accessed | tf_op | source)
XLA Modules:
  0.0 28.8 jit_solution(1707705143847024097)
XLA Ops:
  0.0 1.9 %block_send.1 = (f32[32,8,128]{2,1,0:T(8,128)S(1)}, f32[12,32,128]{2,1,0:T(8,128)S(1)}, f32[4,32,128]{2,1,0:T(8,128)S(1)}, s32[8,128]{1,0:T(8,128)S(1)}) custom-call(f32[2,32,64]{2,1,0:T(8,128)} %refs_0_.1, f32[2,32,64]{2,1,0:T(8,128)} %refs_1_.1, f32[2,32,64]{2,1,0:T(8,128)} %refs_2_.1, f32[2,32,64]{2,1,0:T(8,128)} %refs_3_.1, f32[32,64]{1,0:T(8,128)} %refs_4_.1, ...), custom_call_target="tpu_custom_call" | custom-call | tf_op jit(solution)/shard_map/block_send/pallas_call | solution.py:347
  2.0 15.3 %all_to_all.10 = f32[32,8,128]{2,1,0:T(8,128)S(1)} all-to-all(f32[32,8,128]{2,1,0:T(8,128)S(1)} %get-tuple-element.9), channel_id=1, replica_groups=mesh['lon'=8,'lat'=4] {'lon','lat'}, dimensions={0} | all-to-all | bytes 262144 | tf_op jit(solution)/shard_map/all_to_all | solution.py:574
  17.3 1.3 %column_solve.1 = f32[8,4,2,128]{3,2,1,0:T(2,128)S(1)} custom-call(f32[8,4,8,128]{3,2,1,0:T(8,128)S(1)} %bitcast.2, s32[8,128]{1,0:T(8,128)S(1)} %get-tuple-element.10.turn), custom_call_target="tpu_custom_call" | custom-call | tf_op jit(solution)/shard_map/column_solve/pallas_call | solution.py:347
  18.6 9.0 %all_to_all.11.gathered = f32[32,2,128]{2,1,0:T(2,128)S(1)} all-to-all(f32[32,2,128]{2,1,0:T(2,128)S(1)} %bitcast.3), channel_id=1, replica_groups=mesh['lon'=8,'lat'=4] {'lon','lat'}, dimensions={0} | all-to-all | bytes 65536 | tf_op jit(solution)/shard_map/all_to_all | solution.py:584
  27.6 1.2 %block_close.1 = f32[2,32,64]{2,1,0:T(8,128)} custom-call(f32[32,2,128]{2,1,0:T(2,128)S(1)} %all_to_all.11.gathered, f32[12,32,128]{2,1,0:T(8,128)S(1)} %get-tuple-element.11.factors_ref, f32[4,32,128]{2,1,0:T(8,128)S(1)} %get-tuple-element.12.keep, s32[8,128]{1,0:T(8,128)S(1)} %get-tuple-element.10.turn), custom_call_target="tpu_custom_call" | custom-call | tf_op jit(solution)/shard_map/block_close/pallas_call | solution.py:347
